TPU v7x, 128 devices: a whole 4x4x4 slice. The times are simulated.
128 devices in a mesh: row: 16 (over y, x), col: 8 (over z, core).
Axes of the slice: x: 4, y: 4, z: 4, core: 2. Of those that a mesh axis runs over, the one named last changes fastest.
Arguments:
- features: float32 [32768, 256], P(('row', 'col')), may hold values from -6 to 6
- loader_perm: int32 [32768], P(('row', 'col')), may hold values from 0 to 32767, as said below
- block_values: float32 [16, 8, 256, 4096], P('row', 'col'), may hold values from -0.09375 to 0.09375
- block_row: int32 [16, 8, 256], P('row', 'col'), may hold values from 0 to 63
- block_column: int32 [16, 8, 256], P('row', 'col'), may hold values from 0 to 31
- tile_count: int32 [16, 8], P('row', 'col'), may hold values from 32 to 256, as said below
- weight: float32 [256, 256], replicated, may hold values from -0.375 to 0.375
- bias_vector: float32 [256], replicated, may hold values from -0.5 to 0.5
- cotangent: float32 [32768, 256], P(('row', 'col')), may hold values from -6 to 6
Outputs:
- output: float32 [32768, 256], P(('row', 'col'))
- grad_x: float32 [32768, 256], P(('row', 'col'))
- grad_w: float32 [256, 256], replicated
- grad_b: float32 [256], replicated
Inputs may be any that keep to these rules, and one draw needn't show every extreme that they name: `loader_perm`: every grid position appears once; the 256 loader rows of any one device name the same number of positions, 256 divided by the number of devices, in each aligned block of 256 grid positions. `tile_count`: every count is 256 divided by 1, 2, 4 or 8; a block position may appear in several slots of a tile, and such blocks add.
All inputs are finite; a program needn't handle non-finite values.
Results may differ from a plain program's by a relative error of at most 0.0003.
Values sent between devices are 32-bit elements; how exact they have to be, the bound alone decides.
No kernel may reach another device: no remote copies, remote signals or barrier semaphores. Data moves between devices by JAX's collectives and lax.ppermute only.
A program may use at most 128 MiB of HBM per device.

v0:
```python
import functools
import math

import jax
import jax.numpy as jnp
from jax import lax
from jax.experimental import pallas as pl
from jax.experimental.pallas import tpu as pltpu
from jax.sharding import PartitionSpec as P

precise = lax.Precision.HIGHEST
F = 256
BS = 64
NODE = 256
SLOTS = 256
STEP = 32
DEPTH = 192
ROWS = 16
COLS = 8
SIDE = 4
LANES = 128
W_ROWS = 40


f32 = jnp.float32
bf16 = jnp.bfloat16


def whole():
    return pl.BlockSpec(memory_space=pltpu.VMEM)


def anywhere():
    return pl.BlockSpec(memory_space=pl.ANY)


def row_hop(dy, dx):
    return [
        (y * SIDE + x, (y + dy) % SIDE * SIDE + (x + dx) % SIDE)
        for y in range(SIDE)
        for x in range(SIDE)
    ]


def col_hop(dz, dc):
    return [
        (z * 2 + c, (z + dz) % SIDE * 2 + (c + dc) % 2) for z in range(SIDE) for c in range(2)
    ]


def pack_kernel(features, perm_row, sent):
    owner_row = jnp.broadcast_to(lax.shift_right_logical(perm_row[...], 8), (NODE, NODE))
    owner_col = owner_row.astype(f32).T.astype(jnp.int32)
    first = lax.broadcasted_iota(jnp.int32, (NODE, NODE), 0)
    second = lax.broadcasted_iota(jnp.int32, (NODE, NODE), 1)
    earlier = (owner_col == owner_row) & (first < second)
    rank = jnp.sum(earlier.astype(f32), axis=0, keepdims=True).astype(jnp.int32)
    chosen = (first == owner_row * 2 + rank).astype(f32)
    sent[:, :F] = jnp.dot(chosen, features[...], precision=precise, preferred_element_type=f32)
    place = (perm_row[...] & (NODE - 1)).astype(f32)
    place = jnp.sum(chosen * place, axis=1, keepdims=True)
    sent[:, F:] = jnp.broadcast_to(place, (NODE, LANES))


def pack(features, perm):
    return pl.pallas_call(
        pack_kernel,
        out_shape=jax.ShapeDtypeStruct((NODE, F + LANES), f32),
        in_specs=[whole()] * 2,
        out_specs=whole(),
        name="pack",
    )(features, perm.reshape(1, NODE))


def place_kernel(got, own):
    place = got[:, F:].astype(jnp.int32)
    place = jnp.concatenate([place, place], axis=1)
    second = lax.broadcasted_iota(jnp.int32, (NODE, NODE), 1)
    chosen = (place == second).astype(f32).T
    own[...] = jnp.dot(chosen, got[:, :F], precision=precise, preferred_element_type=f32)


def place(got):
    return pl.pallas_call(
        place_kernel,
        out_shape=jax.ShapeDtypeStruct((NODE, F), f32),
        in_specs=[whole()],
        out_specs=whole(),
        name="place",
    )(got)


def prepare_kernel(flip, count, vals, blocks, lines):
    @pl.when(pl.program_id(0) * STEP < count[0])
    def _():
        for group in range(STEP // 8):
            for tile in range(BS * BS // LANES):
                lines[pl.ds(group * 8 * 32 + tile, 8, stride=32), :] = vals[
                    pl.ds(group * 8, 8), pl.ds(tile * LANES, LANES)
                ]
        left = lax.broadcasted_iota(jnp.int32, (32, LANES), 1) < BS

        def one(slot, carry):
            pair = lines[pl.ds(pl.multiple_of(slot * 32, 32), 32), :]
            turned = pltpu.roll(pair, BS, 1)
            block = jnp.concatenate(
                [jnp.where(left, pair, turned), jnp.where(left, turned, pair)], axis=0
            )
            if flip:
                block = jnp.concatenate([block, block], axis=0).T[:BS]
            high = block.astype(bf16)
            blocks[slot, :, :LANES] = high
            blocks[slot, :, LANES:] = (block - high.astype(f32)).astype(bf16)
            return carry

        lax.fori_loop(0, STEP, one, 0, unroll=8)


def prepare(vals, count, flip):
    def at(step, count):
        return jnp.minimum(step, count[0] // STEP - 1)

    return pl.pallas_call(
        functools.partial(prepare_kernel, flip),
        out_shape=jax.ShapeDtypeStruct((SLOTS, BS, F), bf16),
        grid_spec=pltpu.PrefetchScalarGridSpec(
            num_scalar_prefetch=1,
            grid=(SLOTS // STEP,),
            in_specs=[pl.BlockSpec((STEP, BS * BS), lambda s, n: (at(s, n), 0))],
            out_specs=pl.BlockSpec((STEP, BS, F), lambda s, n: (at(s, n), 0, 0)),
            scratch_shapes=[pltpu.VMEM((STEP * 32, LANES), f32)],
        ),
        cost_estimate=pl.CostEstimate(flops=10**8, bytes_accessed=12 << 20, transcendentals=0),
        name="prepare_back" if flip else "prepare",
    )(count, vals)


def aggregate_kernel(n_src, n_dst, *refs):
    source_at, target_at, count = refs[:3]
    blocks = refs[3]
    sources = refs[4 : 4 + n_src]
    targets = refs[4 + n_src : 4 + n_src + n_dst]
    held, split, total, in_sems, out_sems = refs[4 + n_src + n_dst :]
    step = pl.program_id(0)
    in_rows = sources[0].shape[0]
    out_rows = targets[0].shape[0]

    def load(n):
        return pltpu.make_async_copy(
            sources[n], held.at[pl.ds(n * in_rows, in_rows)], in_sems.at[n]
        )

    def keep(n):
        return pltpu.make_async_copy(
            total.at[pl.ds(n * out_rows, out_rows)], targets[n], out_sems.at[n]
        )

    @pl.when(step == 0)
    def _():
        for n in range(n_src):
            load(n).start()
        total[...] = jnp.zeros_like(total)
        per = in_rows // BS
        for n in range(n_src):
            load(n).wait()

            def one(k, carry):
                at = n * per + k
                rows = held[pl.ds(pl.multiple_of(at * BS, BS), BS), :]
                high = rows.astype(bf16)
                low = (rows - high.astype(f32)).astype(bf16)
                split[at, 0:BS, :] = high
                split[at, BS : 2 * BS, :] = low
                split[at, 2 * BS :, :] = high
                return carry

            lax.fori_loop(0, per, one, 0, unroll=2)

    @pl.when(step * STEP < count[0])
    def _():
        for slot in range(STEP):
            at = step * STEP + slot
            term = jnp.dot(
                blocks[slot][:, :DEPTH], split[source_at[at]], preferred_element_type=f32
            )
            into = pl.ds(pl.multiple_of(target_at[at] * BS, BS), BS)
            total[into, :] += term

    @pl.when(step == pl.num_programs(0) - 1)
    def _():
        for n in range(n_dst):
            keep(n).start()
        for n in range(n_dst):
            keep(n).wait()


def aggregate(blocks, sources, source_at, target_at, count, n_dst, out_rows):
    n_src = len(sources)
    total_in = sum(s.shape[0] for s in sources)
    steps = SLOTS // STEP
    return pl.pallas_call(
        functools.partial(aggregate_kernel, n_src, n_dst),
        out_shape=[jax.ShapeDtypeStruct((out_rows // n_dst, F), f32)] * n_dst,
        grid_spec=pltpu.PrefetchScalarGridSpec(
            num_scalar_prefetch=3,
            grid=(steps,),
            in_specs=[
                pl.BlockSpec(
                    (STEP, BS, F),
                    lambda s, a, b, n: (jnp.minimum(s, n[0] // STEP - 1), 0, 0),
                )
            ]
            + [anywhere()] * n_src,
            out_specs=[anywhere()] * n_dst,
            scratch_shapes=[
                pltpu.VMEM((total_in, F), f32),
                pltpu.VMEM((total_in // BS, DEPTH, F), bf16),
                pltpu.VMEM((out_rows, F), f32),
                pltpu.SemaphoreType.DMA((n_src,)),
                pltpu.SemaphoreType.DMA((n_dst,)),
            ],
        ),
        cost_estimate=pl.CostEstimate(
            flops=2 * SLOTS * BS * F * F, bytes_accessed=16 << 20, transcendentals=0
        ),
    )(source_at, target_at, count, blocks, *sources)


def middle_kernel(*refs):
    parts, (weight, bias, cotangent) = refs[:8], refs[8:11]
    output, grad_a, grad_b, sums, hidden, turned, strip = refs[11:]
    half = NODE // 2
    hidden[:half] = parts[0][...] + parts[1][...] + parts[2][...] + parts[3][...]
    hidden[half:] = parts[4][...] + parts[5][...] + parts[6][...] + parts[7][...]
    for side in range(2):
        lanes = slice(side * LANES, (side + 1) * LANES)
        strip[side * NODE : (side + 1) * NODE] = cotangent[:, lanes]
        for q in range(NODE // BS):
            for odd in range(2):
                turned[pl.ds(q * BS + odd * 32, 32), lanes] = strip[
                    pl.ds(side * NODE + q * BS + odd, 32, stride=2), :
                ]
    rows = hidden[...]
    preact = jnp.dot(rows, weight[...], precision=precise, preferred_element_type=f32)
    preact = preact + bias[...]
    squashed = 1.0 / (1.0 + jnp.exp(-preact))
    grad_pre = turned[...] * squashed * (1.0 + preact * (1.0 - squashed))
    turned[...] = preact * squashed
    grad = lax.dot_general(
        grad_pre, weight[...], (((1,), (1,)), ((), ())), precision=precise,
        preferred_element_type=f32,
    )
    grad_a[...] = grad[:half]
    grad_b[...] = grad[half:]
    for side in range(2):
        lanes = slice(side * LANES, (side + 1) * LANES)
        for q in range(NODE // BS):
            for odd in range(2):
                strip[pl.ds(side * NODE + q * BS + odd, 32, stride=2), :] = turned[
                    pl.ds(q * BS + odd * 32, 32), lanes
                ]
        output[:, lanes] = strip[side * NODE : (side + 1) * NODE]
    local_w = jnp.dot(rows.T, grad_pre, precision=precise, preferred_element_type=f32)
    local_b = jnp.sum(grad_pre, axis=0, keepdims=True)
    for n in range(COLS):
        sums[n, 0:32, :] = local_w[n * 32 : (n + 1) * 32]
        sums[n, 32:, :] = jnp.broadcast_to(local_b, (W_ROWS - 32, F))


def middle(parts, weight, bias, cotangent):
    return pl.pallas_call(
        middle_kernel,
        out_shape=[
            jax.ShapeDtypeStruct((NODE, F), f32),
            jax.ShapeDtypeStruct((NODE // 2, F), f32),
            jax.ShapeDtypeStruct((NODE // 2, F), f32),
            jax.ShapeDtypeStruct((COLS, W_ROWS, F), f32),
        ],
        in_specs=[whole()] * 11,
        out_specs=[whole()] * 4,
        scratch_shapes=[pltpu.VMEM((NODE, F), f32)] * 2 + [pltpu.VMEM((2 * NODE, LANES), f32)],
        name="middle",
    )(*parts, weight, bias.reshape(1, F), cotangent)


def on_device(
    features,
    loader_perm,
    block_values,
    block_row,
    block_column,
    tile_count,
    weight,
    bias_vector,
    cotangent,
):
    row = lax.axis_index("row")
    col = lax.axis_index("col")
    my_y, my_x = row // SIDE, row % SIDE
    my_z, my_c = col // 2, col % 2
    count = tile_count.reshape(1)
    tile_rows = block_row.reshape(SLOTS)
    tile_columns = block_column.reshape(SLOTS)

    r_dev, r_q = tile_rows >> 2, tile_rows & 3
    r_y, r_x = r_dev >> 2, r_dev & 3
    c_dev, c_q = tile_columns >> 2, tile_columns & 3
    c_z, c_c = c_dev >> 1, c_dev & 1
    out_d, out_e = (r_x - my_x) & 3, (r_y - my_y) & 3
    in_d, in_e = (my_x - r_x) & 3, (my_y - r_y) & 3

    def row_slot(d, e):
        first = d * 8 + e * 2 + (r_q & 1)
        second = 32 + e * 8 + d * 2 + (r_q & 1)
        return jnp.where(r_q < 2, first, second)

    fwd_to = row_slot(out_d, out_e)
    bwd_from = row_slot(in_d, in_e)
    other = c_c ^ my_c
    fwd_from = (((my_z - c_z) & 3) * 2 + other) * 4 + c_q
    bwd_to = (other * 4 + ((c_z - my_z) & 3)) * 4 + c_q

    sent = pack(features, loader_perm).reshape(ROWS * COLS, 2, F + LANES)
    got = lax.all_to_all(sent, ("row", "col"), split_axis=0, concat_axis=0, tiled=True)
    vals = block_values.reshape(SLOTS, BS * BS)
    fwd_blocks = prepare(vals, count, False)
    got, fwd_blocks = lax.optimization_barrier((got, fwd_blocks))
    own = place(got.reshape(NODE, F + LANES))
    panel = [own] + [lax.ppermute(own, "col", col_hop(f, 0)) for f in (1, 2, 3)]
    sources = []
    for part in panel:
        sources += [part, lax.ppermute(part, "col", col_hop(0, 1))]

    half = list(aggregate(
        fwd_blocks, sources, fwd_from, fwd_to, count, 8, ROWS * NODE)
    )
    got_a = [lax.ppermute(half[d], "row", row_hop(0, d)) for d in (1, 2, 3)]
    got_b = [lax.ppermute(half[4 + e], "row", row_hop(e, 0)) for e in (1, 2, 3)]
    n = NODE // 2
    back_count, half[0] = lax.optimization_barrier((count, half[0]))
    bwd_blocks = prepare(vals, back_count, True)
    got_a[0], bwd_blocks = lax.optimization_barrier((got_a[0], bwd_blocks))

    def partial(own_part, got, k):
        cut = slice(k * n, (k + 1) * n)
        return own_part[cut] + got[0][cut] + got[1][cut] + got[2][cut]

    sum_a = [partial(half[0], got_a, k) for k in range(SIDE)]
    sum_b = [partial(half[4], got_b, k) for k in range(SIDE)]
    parts = [sum_a[0]] + [lax.ppermute(sum_a[e], "row", row_hop(e, 0)) for e in (1, 2, 3)]
    parts += [sum_b[0]] + [lax.ppermute(sum_b[d], "row", row_hop(0, d)) for d in (1, 2, 3)]

    output, grad_a, grad_b, sums = middle(parts, weight, bias_vector, cotangent)

    near_a = [grad_a] + [lax.ppermute(grad_a, "row", row_hop(e, 0)) for e in (1, 2, 3)]
    near_b = [grad_b] + [lax.ppermute(grad_b, "row", row_hop(0, d)) for d in (1, 2, 3)]
    near_a = jnp.concatenate(near_a, axis=0)
    near_b = jnp.concatenate(near_b, axis=0)
    column = [near_a] + [lax.ppermute(near_a, "row", row_hop(0, d)) for d in (1, 2, 3)]
    column += [near_b] + [lax.ppermute(near_b, "row", row_hop(e, 0)) for e in (1, 2, 3)]

    sums = lax.all_to_all(sums, "col", split_axis=0, concat_axis=0, tiled=True)
    sums = jnp.sum(sums, axis=0)
    sums = jnp.broadcast_to(sums[None], (ROWS, W_ROWS, F))
    bwd_from, sums = lax.optimization_barrier((bwd_from, sums))
    sums = lax.all_to_all(sums, "row", split_axis=0, concat_axis=0, tiled=True)
    keep, give = aggregate(bwd_blocks, column, bwd_from, bwd_to, count, 2, COLS * NODE)
    taken = lax.ppermute(give, "col", col_hop(0, 1))
    keep, sums = lax.optimization_barrier((keep, sums))
    sums_x = [
        keep[k * NODE : (k + 1) * NODE] + taken[k * NODE : (k + 1) * NODE] for k in range(SIDE)
    ]
    got_x = [lax.ppermute(sums_x[f], "col", col_hop(f, 0)) for f in (1, 2, 3)]
    norm_scale = 1.0 / math.sqrt(NODE * ROWS * COLS)
    sums = jnp.sum(sums, axis=0) * norm_scale
    sums = jnp.broadcast_to(sums[None], (COLS, W_ROWS, F))
    sums = lax.all_to_all(sums, "col", split_axis=0, concat_axis=0, tiled=True)
    grad_w = sums[:, :32].reshape(F, F)
    grad_bias = sums[0, 32]
    grad_x = sums_x[0] + got_x[0] + got_x[1] + got_x[2]
    return (output, grad_x, grad_w, grad_bias)


def solution(mesh):
    in_specs = (
        P(("row", "col"), None),
        P(("row", "col")),
        P("row", "col", None, None),
        P("row", "col", None),
        P("row", "col", None),
        P("row", "col"),
        P(),
        P(),
        P(("row", "col"), None),
    )
    out_specs = (P(("row", "col"), None), P(("row", "col"), None), P(), P())

    return jax.shard_map(
        on_device, mesh=mesh, in_specs=in_specs, out_specs=out_specs, check_vma=False
    )
```

profile of v0, /device:TPU:0, one launch (start us, length us, event | category | flops | bytes accessed | tf_op | source)
XLA Modules:
  0.0 237.0 jit_solution(18165842144081774719)
XLA Ops:
  0.7 2.2 pack.1
  2.8 2.0 reshape.83
  4.8 11.2 %all-to-all-start = ((f32[128,2,384]{2,1,0:T(2,128)}), f32[128,2,384]{2,1,0:T(2,128)S(1)}, u32[]{:S(2)}, u32[]{:S(2)}) async-start(f32[128,2,384]{2,1,0:T(2,128)} %reshape.83), calls=%async_computation | async-start | bytes 786432 | tf_op jit(solution)/shard_map/all_to_all | solution.py:324
  16.6 3.2 %prepare.1.refs_3_ = bf16[256,64,256]{2,1,0:T(8,128)(2,1)} custom-call(s32[1]{0:T(128)} %bitcast.11.count, f32[256,4096]{1,0:T(8,128)} %bitcast.14), custom_call_target="tpu_custom_call" | custom-call | flops 100000000 | bytes 12582912 | tf_op jit(solution)/shard_map/prepare/pallas_call | solution.py:123
  19.9 8.4 %all-to-all-done = f32[128,2,384]{2,1,0:T(2,128)S(1)} async-done(((f32[128,2,384]{2,1,0:T(2,128)}), f32[128,2,384]{2,1,0:T(2,128)S(1)}, u32[]{:S(2)}, u32[]{:S(2)}) %all-to-all-start) | async-done | bytes 393248 | tf_op jit(solution)/shard_map/all_to_all | solution.py:324
  28.3 1.0 reshape.85.got
  29.3 2.1 place.1.refs_4_
  31.7 2.9 %collective-permute-start.3 = (f32[256,256]{1,0:T(8,128)}, f32[256,256]{1,0:T(8,128)S(1)}, u32[]{:S(2)}, u32[]{:S(2)}) collective-permute-start(f32[256,256]{1,0:T(8,128)} %place.1.refs_4_), channel_id=1, source_target_pairs={{0,4},{1,5},{2,6},{3,7},{4,0},{5,1},{6,2},{7,3},{8,12},{9,13},{10,... | collective-permute-start | bytes 786440 | tf_op jit(solution)/shard_map/ppermute | solution.py:329
  35.1 10.9 %collective-permute-done.1.refs_6_ = f32[256,256]{1,0:T(8,128)S(1)} collective-permute-done((f32[256,256]{1,0:T(8,128)}, f32[256,256]{1,0:T(8,128)S(1)}, u32[]{:S(2)}, u32[]{:S(2)}) %collective-permute-start.1) | collective-permute-done | bytes 262176 | tf_op jit(solution)/shard_map/ppermute | solution.py:329
  49.0 6.8 %shard_map.120 = (f32[512,256]{1,0:T(8,128)}, f32[512,256]{1,0:T(8,128)}, f32[512,256]{1,0:T(8,128)}, f32[512,256]{1,0:T(8,128)}, f32[512,256]{1,0:T(8,128)}, /*...) custom-call(s32[256]{0:T(256)} %bitcast.18, s32[256]{0:T(256)} %bitcast.17, s32[1]{0:T(128)} %bitcast.12.refs_2_, ...), custom_call_target="tpu_custom_call" | custom-call | flops 2147483648 | bytes 16777216 | tf_op jit(solution)/shard_map/pallas_call | solution.py:201
  55.8 7.3 %collective-permute-start.13 = (f32[512,256]{1,0:T(8,128)}, f32[512,256]{1,0:T(8,128)S(1)}, u32[]{:S(2)}, u32[]{:S(2)}) collective-permute-start(f32[512,256]{1,0:T(8,128)} %get-tuple-element.38), channel_id=1, source_target_pairs={{0,32},{8,40},{16,48},{24,56},{32,64},{40,72},{48,80},{56,88},{64,... | collective-permute-start | bytes 1572872 | tf_op jit(solution)/shard_map/ppermute | solution.py:338
  63.1 2.8 %collective-permute-start.15 = (f32[512,256]{1,0:T(8,128)}, f32[512,256]{1,0:T(8,128)}, u32[]{:S(2)}, u32[]{:S(2)}) collective-permute-start(f32[512,256]{1,0:T(8,128)} %get-tuple-element.40), channel_id=1, source_target_pairs={{0,96},{8,104},{16,112},{24,120},{32,0},{40,8},{48,16},{56,24},{64... | collective-permute-start | bytes 1572872 | tf_op jit(solution)/shard_map/ppermute | solution.py:338
  66.2 2.6 %collective-permute-start.8 = (f32[512,256]{1,0:T(8,128)}, f32[512,256]{1,0:T(8,128)S(1)}, u32[]{:S(2)}, u32[]{:S(2)}) collective-permute-start(f32[512,256]{1,0:T(8,128)} %get-tuple-element.35), channel_id=1, source_target_pairs={{0,16},{8,24},{16,0},{24,8},{32,48},{40,56},{48,32},{56,40},{64,80... | collective-permute-start | bytes 1572872 | tf_op jit(solution)/shard_map/ppermute | solution.py:337
  68.8 6.9 %collective-permute-done.13 = f32[512,256]{1,0:T(8,128)S(1)} collective-permute-done((f32[512,256]{1,0:T(8,128)}, f32[512,256]{1,0:T(8,128)S(1)}, u32[]{:S(2)}, u32[]{:S(2)}) %collective-permute-start.13) | collective-permute-done | bytes 524320 | tf_op jit(solution)/shard_map/ppermute | solution.py:338
  75.7 3.4 %collective-permute-start.9 = (f32[512,256]{1,0:T(8,128)}, f32[512,256]{1,0:T(8,128)S(1)}, u32[]{:S(2)}, u32[]{:S(2)}) collective-permute-start(f32[512,256]{1,0:T(8,128)} %get-tuple-element.36), channel_id=1, source_target_pairs={{0,24},{8,0},{16,8},{24,16},{32,56},{40,32},{48,40},{56,48},{64,88... | collective-permute-start | bytes 1572872 | tf_op jit(solution)/shard_map/ppermute | solution.py:337
  79.1 3.8 %prepare_back.1.refs_3_ = bf16[256,64,256]{2,1,0:T(8,128)(2,1)} custom-call(s32[1]{0:T(128)} %bitcast.10.count, f32[256,4096]{1,0:T(8,128)} %bitcast.15), custom_call_target="tpu_custom_call" | custom-call | flops 100000000 | bytes 12582912 | tf_op jit(solution)/shard_map/prepare_back/pallas_call | solution.py:123
  82.9 3.4 %collective-permute-done.14 = f32[512,256]{1,0:T(8,128)} collective-permute-done((f32[512,256]{1,0:T(8,128)}, f32[512,256]{1,0:T(8,128)}, u32[]{:S(2)}, u32[]{:S(2)}) %collective-permute-start.14) | collective-permute-done | bytes 524320 | tf_op jit(solution)/shard_map/ppermute | solution.py:338
  86.9 2.1 slice_add_fusion.4
  88.9 16.0 %collective-permute-start.16 = (f32[128,256]{1,0:T(8,128)S(1)}, f32[128,256]{1,0:T(8,128)S(1)}, u32[]{:S(2)}, u32[]{:S(2)}) collective-permute-start(f32[128,256]{1,0:T(8,128)S(1)} %get-tuple-element.57), channel_id=1, source_target_pairs={{0,8},{8,16},{16,24},{24,0},{32,40},{40,48},{48,56},{56,32},{64,72... | collective-permute-start | bytes 393224 | tf_op jit(solution)/shard_map/ppermute | solution.py:351
  105.0 2.7 %collective-permute-start.18 = (f32[128,256]{1,0:T(8,128)S(1)}, f32[128,256]{1,0:T(8,128)S(1)}, u32[]{:S(2)}, u32[]{:S(2)}) collective-permute-start(f32[128,256]{1,0:T(8,128)S(1)} %get-tuple-element.55), channel_id=1, source_target_pairs={{0,24},{8,0},{16,8},{24,16},{32,56},{40,32},{48,40},{56,48},{64,88... | collective-permute-start | bytes 393224 | tf_op jit(solution)/shard_map/ppermute | solution.py:351
  108.4 3.1 %collective-permute-start.11 = (f32[128,256]{1,0:T(8,128)S(1)}, f32[128,256]{1,0:T(8,128)S(1)}, u32[]{:S(2)}, u32[]{:S(2)}) collective-permute-start(f32[128,256]{1,0:T(8,128)S(1)} %get-tuple-element.60), channel_id=1, source_target_pairs={{0,64},{8,72},{16,80},{24,88},{32,96},{40,104},{48,112},{56,120},{... | collective-permute-start | bytes 393224 | tf_op jit(solution)/shard_map/ppermute | solution.py:350
  111.9 2.7 %collective-permute-done.10.refs_1_ = f32[128,256]{1,0:T(8,128)S(1)} collective-permute-done((f32[128,256]{1,0:T(8,128)S(1)}, f32[128,256]{1,0:T(8,128)S(1)}, u32[]{:S(2)}, u32[]{:S(2)}) %collective-permute-start.10) | collective-permute-done | bytes 131104 | tf_op jit(solution)/shard_map/ppermute | solution.py:350
  114.6 1.4 collective-permute-done.11.refs_2_
  117.6 3.3 %middle.1 = (f32[256,256]{1,0:T(8,128)}, f32[128,256]{1,0:T(8,128)}, f32[128,256]{1,0:T(8,128)}, f32[8,40,256]{2,1,0:T(8,128)}) custom-call(f32[128,256]{1,0:T(8,128)} %get-tuple-element.62.refs_0_, f32[128,256]{1,0:T(8,128)} %copy-done.17, f32[128,256]{1,0:T(8,128)} %copy-done.18, f32[128,256]{1,0:T(8,128)} %copy-done.19, ...), custom_call_target="tpu_custom_call" | custom-call | tf_op jit(solution)/shard_map/middle/pallas_call | solution.py:271
  120.9 2.9 %collective-permute-start.26 = (f32[128,256]{1,0:T(8,128)}, f32[128,256]{1,0:T(8,128)S(1)}, u32[]{:S(2)}, u32[]{:S(2)}) collective-permute-start(f32[128,256]{1,0:T(8,128)} %get-tuple-element.46), channel_id=1, source_target_pairs={{0,16},{8,24},{16,0},{24,8},{32,48},{40,56},{48,32},{56,40},{64,80... | collective-permute-start | bytes 393224 | tf_op jit(solution)/shard_map/ppermute | solution.py:356
  125.3 3.3 %collective-permute-done.25 = f32[128,256]{1,0:T(8,128)S(1)} collective-permute-done((f32[128,256]{1,0:T(8,128)}, f32[128,256]{1,0:T(8,128)S(1)}, u32[]{:S(2)}, u32[]{:S(2)}) %collective-permute-start.25) | collective-permute-done | bytes 131104 | tf_op jit(solution)/shard_map/ppermute | solution.py:356
  128.7 1.2 collective-permute-done.27
  130.7 4.0 %collective-permute-start.20 = (f32[128,256]{1,0:T(8,128)}, f32[128,256]{1,0:T(8,128)S(1)}, u32[]{:S(2)}, u32[]{:S(2)}) collective-permute-start(f32[128,256]{1,0:T(8,128)} %get-tuple-element.45), channel_id=1, source_target_pairs={{0,64},{8,72},{16,80},{24,88},{32,96},{40,104},{48,112},{56,120},{... | collective-permute-start | bytes 393224 | tf_op jit(solution)/shard_map/ppermute | solution.py:355
  134.7 0.9 constant_dynamic-update-slice_fusion.3
  135.7 2.1 collective-permute-start.21
  137.8 10.9 %collective-permute-done.19 = f32[128,256]{1,0:T(8,128)S(1)} collective-permute-done((f32[128,256]{1,0:T(8,128)}, f32[128,256]{1,0:T(8,128)S(1)}, u32[]{:S(2)}, u32[]{:S(2)}) %collective-permute-start.19) | collective-permute-done | bytes 131104 | tf_op jit(solution)/shard_map/ppermute | solution.py:355
  148.6 1.6 collective-permute-start.30
  151.1 2.5 %collective-permute-start.22 = (f32[512,256]{1,0:T(8,128)S(1)}, f32[512,256]{1,0:T(8,128)}, u32[]{:S(2)}, u32[]{:S(2)}) collective-permute-start(f32[512,256]{1,0:T(8,128)S(1)} %constant_dynamic-update-slice_fusion.refs_4_), channel_id=1, source_target_pairs={{0,8},{8,16},{16,24},{24,0},{32,40},{40,48},{48,56},{56,32},{64,72... | collective-permute-start | bytes 1572872 | tf_op jit(solution)/shard_map/ppermute | solution.py:359
  153.6 1.4 collective-permute-start.23
  155.0 1.4 collective-permute-start.24
  156.4 16.0 %all_to_all.20 = f32[8,40,256]{2,1,0:T(8,128)S(1)} all-to-all(f32[8,40,256]{2,1,0:T(8,128)} %get-tuple-element.42), channel_id=1, replica_groups=mesh['row'=16,'col'=8] {'col'}, dimensions={0} | all-to-all | bytes 655360 | tf_op jit(solution)/shard_map/all_to_all | solution.py:362
  173.5 6.6 %shard_map.121 = (f32[1024,256]{1,0:T(8,128)}, f32[1024,256]{1,0:T(8,128)}) custom-call(s32[256]{0:T(256)} %bitcast.19, s32[256]{0:T(256)} %bitcast.20, s32[1]{0:T(128)} %bitcast.13.refs_2_, bf16[256,64,256]{2,1,0:T(8,128)(2,1)} %prepare_back.1.refs_3_, f32[512,256]{1,0:T(8,128)} %copy-done, f32[512,256]{1,0:T(8,128)} %collective-permute-done.22.refs_5_, ...), custom_call_target="tpu_custom_call" | custom-call | flops 2147483648 | bytes 16777216 | tf_op jit(solution)/shard_map/pallas_call | solution.py:201
  180.0 2.6 %collective-permute-start.31 = (f32[1024,256]{1,0:T(8,128)}, f32[1024,256]{1,0:T(8,128)S(1)}, u32[]{:S(2)}, u32[]{:S(2)}) collective-permute-start(f32[1024,256]{1,0:T(8,128)} %get-tuple-element.50), channel_id=1, source_target_pairs={{0,1},{1,0},{2,3},{3,2},{4,5},{5,4},{6,7},{7,6},{8,9},{9,8},{10,11... | collective-permute-start | bytes 3145736 | tf_op jit(solution)/shard_map/ppermute | solution.py:368
  182.6 24.8 %all_to_all.21 = f32[16,40,256]{2,1,0:T(8,128)S(1)} all-to-all(f32[16,40,256]{2,1,0:T(8,128)S(1)} %broadcast_in_dim.4), channel_id=1, replica_groups=mesh['row'=16,'col'=8] {'row'}, dimensions={0} | all-to-all | bytes 1310720 | tf_op jit(solution)/shard_map/all_to_all | solution.py:366
  208.2 7.7 %all-to-all-start.3 = ((f32[8,40,256]{2,1,0:T(8,128)}), f32[8,40,256]{2,1,0:T(8,128)S(1)}, u32[]{:S(2)}, u32[]{:S(2)}) async-start(f32[8,40,256]{2,1,0:T(8,128)} %broadcast_in_dim.5), calls=%async_computation.3 | async-start | bytes 655360 | tf_op jit(solution)/shard_map/all_to_all | solution.py:377
  215.8 1.2 slice_add_fusion.2
  217.1 2.1 collective-permute-start.32
  219.1 2.7 %collective-permute-start.33 = (f32[256,256]{1,0:T(8,128)S(1)}, f32[256,256]{1,0:T(8,128)S(1)}, u32[]{:S(2)}, u32[]{:S(2)}) collective-permute-start(f32[256,256]{1,0:T(8,128)S(1)} %get-tuple-element.54), channel_id=1, source_target_pairs={{0,4},{1,5},{2,6},{3,7},{4,0},{5,1},{6,2},{7,3},{8,12},{9,13},{10,... | collective-permute-start | bytes 786440 | tf_op jit(solution)/shard_map/ppermute | solution.py:373
  221.8 1.5 collective-permute-start.34
  223.3 1.3 all-to-all-done.3
  225.9 3.7 %collective-permute-done.32 = f32[256,256]{1,0:T(8,128)S(1)} collective-permute-done((f32[256,256]{1,0:T(8,128)S(1)}, f32[256,256]{1,0:T(8,128)S(1)}, u32[]{:S(2)}, u32[]{:S(2)}) %collective-permute-start.32) | collective-permute-done | bytes 262176 | tf_op jit(solution)/shard_map/ppermute | solution.py:373
  229.6 5.6 %collective-permute-done.33 = f32[256,256]{1,0:T(8,128)S(1)} collective-permute-done((f32[256,256]{1,0:T(8,128)S(1)}, f32[256,256]{1,0:T(8,128)S(1)}, u32[]{:S(2)}, u32[]{:S(2)}) %collective-permute-start.33) | collective-permute-done | bytes 262176 | tf_op jit(solution)/shard_map/ppermute | solution.py:373
  235.3 1.7 fusion.2
  (102 shorter events, 13.8 us)
Async XLA Ops:
  0.6 46.0 %copy-start.20 = (s32[1,1,256]{2,1,0:T(1,128)S(1)}, s32[1,1,256]{2,1,0:T(1,128)}, u32[]{:S(2)}) copy-start(s32[1,1,256]{2,1,0:T(1,128)} %param.12) | copy-start | bytes 3076
  0.6 46.6 %copy-start.21 = (s32[1,1,256]{2,1,0:T(1,128)S(1)}, s32[1,1,256]{2,1,0:T(1,128)}, u32[]{:S(2)}) copy-start(s32[1,1,256]{2,1,0:T(1,128)} %param.13) | copy-start | bytes 3076
  4.8 23.5 %all-to-all-start = ((f32[128,2,384]{2,1,0:T(2,128)}), f32[128,2,384]{2,1,0:T(2,128)S(1)}, u32[]{:S(2)}, u32[]{:S(2)}) async-start(f32[128,2,384]{2,1,0:T(2,128)} %reshape.83), calls=%async_computation | async-start | bytes 786432 | tf_op jit(solution)/shard_map/all_to_all | solution.py:324
  31.4 14.6 %collective-permute-start.1 = (f32[256,256]{1,0:T(8,128)}, f32[256,256]{1,0:T(8,128)S(1)}, u32[]{:S(2)}, u32[]{:S(2)}) collective-permute-start(f32[256,256]{1,0:T(8,128)} %place.1.refs_4_), channel_id=1, source_target_pairs={{0,2},{1,3},{2,4},{3,5},{4,6},{5,7},{6,0},{7,1},{8,10},{9,11},{10,... | collective-permute-start | bytes 786440 | tf_op jit(solution)/shard_map/ppermute | solution.py:329
  31.7 14.3 %collective-permute-start.3 = (f32[256,256]{1,0:T(8,128)}, f32[256,256]{1,0:T(8,128)S(1)}, u32[]{:S(2)}, u32[]{:S(2)}) collective-permute-start(f32[256,256]{1,0:T(8,128)} %place.1.refs_4_), channel_id=1, source_target_pairs={{0,4},{1,5},{2,6},{3,7},{4,0},{5,1},{6,2},{7,3},{8,12},{9,13},{10,... | collective-permute-start | bytes 786440 | tf_op jit(solution)/shard_map/ppermute | solution.py:329
  34.6 12.0 %collective-permute-start.5 = (f32[256,256]{1,0:T(8,128)}, f32[256,256]{1,0:T(8,128)S(1)}, u32[]{:S(2)}, u32[]{:S(2)}) collective-permute-start(f32[256,256]{1,0:T(8,128)} %place.1.refs_4_), channel_id=1, source_target_pairs={{0,6},{1,7},{2,0},{3,1},{4,2},{5,3},{6,4},{7,5},{8,14},{9,15},{10,... | collective-permute-start | bytes 786440 | tf_op jit(solution)/shard_map/ppermute | solution.py:329
  34.8 13.0 %collective-permute-start = (f32[256,256]{1,0:T(8,128)}, f32[256,256]{1,0:T(8,128)S(1)}, u32[]{:S(2)}, u32[]{:S(2)}) collective-permute-start(f32[256,256]{1,0:T(8,128)} %place.1.refs_4_), channel_id=1, source_target_pairs={{0,1},{1,0},{2,3},{3,2},{4,5},{5,4},{6,7},{7,6},{8,9},{9,8},{10,11... | collective-permute-start | bytes 786440 | tf_op jit(solution)/shard_map/ppermute | solution.py:332
  46.0 1.9 collective-permute-start.2
  46.0 1.9 collective-permute-start.4
  46.6 1.7 collective-permute-start.6
  55.8 31.1 %copy-start.3 = (f32[512,256]{1,0:T(8,128)S(1)}, f32[512,256]{1,0:T(8,128)}, u32[]{:S(2)}) copy-start(f32[512,256]{1,0:T(8,128)} %get-tuple-element.37) | copy-start | bytes 1572868
  55.8 51.9 %copy-start.2 = (f32[512,256]{1,0:T(8,128)S(1)}, f32[512,256]{1,0:T(8,128)}, u32[]{:S(2)}) copy-start(f32[512,256]{1,0:T(8,128)} %get-tuple-element.31) | copy-start | bytes 1572868
  55.8 19.9 %collective-permute-start.13 = (f32[512,256]{1,0:T(8,128)}, f32[512,256]{1,0:T(8,128)S(1)}, u32[]{:S(2)}, u32[]{:S(2)}) collective-permute-start(f32[512,256]{1,0:T(8,128)} %get-tuple-element.38), channel_id=1, source_target_pairs={{0,32},{8,40},{16,48},{24,56},{32,64},{40,72},{48,80},{56,88},{64,... | collective-permute-start | bytes 1572872 | tf_op jit(solution)/shard_map/ppermute | solution.py:338
  63.1 23.2 %collective-permute-start.14 = (f32[512,256]{1,0:T(8,128)}, f32[512,256]{1,0:T(8,128)}, u32[]{:S(2)}, u32[]{:S(2)}) collective-permute-start(f32[512,256]{1,0:T(8,128)} %get-tuple-element.39), channel_id=1, source_target_pairs={{0,64},{8,72},{16,80},{24,88},{32,96},{40,104},{48,112},{56,120},{... | collective-permute-start | bytes 1572872 | tf_op jit(solution)/shard_map/ppermute | solution.py:338
  63.1 23.8 %collective-permute-start.15 = (f32[512,256]{1,0:T(8,128)}, f32[512,256]{1,0:T(8,128)}, u32[]{:S(2)}, u32[]{:S(2)}) collective-permute-start(f32[512,256]{1,0:T(8,128)} %get-tuple-element.40), channel_id=1, source_target_pairs={{0,96},{8,104},{16,112},{24,120},{32,0},{40,8},{48,16},{56,24},{64... | collective-permute-start | bytes 1572872 | tf_op jit(solution)/shard_map/ppermute | solution.py:338
  65.8 39.1 %collective-permute-start.7 = (f32[512,256]{1,0:T(8,128)}, f32[512,256]{1,0:T(8,128)S(1)}, u32[]{:S(2)}, u32[]{:S(2)}) collective-permute-start(f32[512,256]{1,0:T(8,128)} %get-tuple-element.32), channel_id=1, source_target_pairs={{0,8},{8,16},{16,24},{24,0},{32,40},{40,48},{48,56},{56,32},{64,72... | collective-permute-start | bytes 1572872 | tf_op jit(solution)/shard_map/ppermute | solution.py:337
  66.2 41.4 %collective-permute-start.8 = (f32[512,256]{1,0:T(8,128)}, f32[512,256]{1,0:T(8,128)S(1)}, u32[]{:S(2)}, u32[]{:S(2)}) collective-permute-start(f32[512,256]{1,0:T(8,128)} %get-tuple-element.35), channel_id=1, source_target_pairs={{0,16},{8,24},{16,0},{24,8},{32,48},{40,56},{48,32},{56,40},{64,80... | collective-permute-start | bytes 1572872 | tf_op jit(solution)/shard_map/ppermute | solution.py:337
  75.7 31.9 %collective-permute-start.9 = (f32[512,256]{1,0:T(8,128)}, f32[512,256]{1,0:T(8,128)S(1)}, u32[]{:S(2)}, u32[]{:S(2)}) collective-permute-start(f32[512,256]{1,0:T(8,128)} %get-tuple-element.36), channel_id=1, source_target_pairs={{0,24},{8,0},{16,8},{24,16},{32,56},{40,32},{48,40},{56,48},{64,88... | collective-permute-start | bytes 1572872 | tf_op jit(solution)/shard_map/ppermute | solution.py:337
  88.9 22.6 %collective-permute-start.16 = (f32[128,256]{1,0:T(8,128)S(1)}, f32[128,256]{1,0:T(8,128)S(1)}, u32[]{:S(2)}, u32[]{:S(2)}) collective-permute-start(f32[128,256]{1,0:T(8,128)S(1)} %get-tuple-element.57), channel_id=1, source_target_pairs={{0,8},{8,16},{16,24},{24,0},{32,40},{40,48},{48,56},{56,32},{64,72... | collective-permute-start | bytes 393224 | tf_op jit(solution)/shard_map/ppermute | solution.py:351
  104.9 7.0 %collective-permute-start.17 = (f32[128,256]{1,0:T(8,128)S(1)}, f32[128,256]{1,0:T(8,128)S(1)}, u32[]{:S(2)}, u32[]{:S(2)}) collective-permute-start(f32[128,256]{1,0:T(8,128)S(1)} %get-tuple-element.56), channel_id=1, source_target_pairs={{0,16},{8,24},{16,0},{24,8},{32,48},{40,56},{48,32},{56,40},{64,80... | collective-permute-start | bytes 393224 | tf_op jit(solution)/shard_map/ppermute | solution.py:351
  105.0 7.0 %collective-permute-start.18 = (f32[128,256]{1,0:T(8,128)S(1)}, f32[128,256]{1,0:T(8,128)S(1)}, u32[]{:S(2)}, u32[]{:S(2)}) collective-permute-start(f32[128,256]{1,0:T(8,128)S(1)} %get-tuple-element.55), channel_id=1, source_target_pairs={{0,24},{8,0},{16,8},{24,16},{32,56},{40,32},{48,40},{56,48},{64,88... | collective-permute-start | bytes 393224 | tf_op jit(solution)/shard_map/ppermute | solution.py:351
  108.4 6.2 %collective-permute-start.10 = (f32[128,256]{1,0:T(8,128)S(1)}, f32[128,256]{1,0:T(8,128)S(1)}, u32[]{:S(2)}, u32[]{:S(2)}) collective-permute-start(f32[128,256]{1,0:T(8,128)S(1)} %get-tuple-element.61), channel_id=1, source_target_pairs={{0,32},{8,40},{16,48},{24,56},{32,64},{40,72},{48,80},{56,88},{64,... | collective-permute-start | bytes 393224 | tf_op jit(solution)/shard_map/ppermute | solution.py:350
  108.4 7.6 %collective-permute-start.11 = (f32[128,256]{1,0:T(8,128)S(1)}, f32[128,256]{1,0:T(8,128)S(1)}, u32[]{:S(2)}, u32[]{:S(2)}) collective-permute-start(f32[128,256]{1,0:T(8,128)S(1)} %get-tuple-element.60), channel_id=1, source_target_pairs={{0,64},{8,72},{16,80},{24,88},{32,96},{40,104},{48,112},{56,120},{... | collective-permute-start | bytes 393224 | tf_op jit(solution)/shard_map/ppermute | solution.py:350
  111.6 5.4 %copy-start.14 = (f32[128,256]{1,0:T(8,128)}, f32[128,256]{1,0:T(8,128)S(1)}, u32[]{:S(2)}) copy-start(f32[128,256]{1,0:T(8,128)S(1)} %collective-permute-done.16.refs_5_) | copy-start | bytes 393220
  111.6 5.4 %collective-permute-start.12 = (f32[128,256]{1,0:T(8,128)S(1)}, f32[128,256]{1,0:T(8,128)S(1)}, u32[]{:S(2)}, u32[]{:S(2)}) collective-permute-start(f32[128,256]{1,0:T(8,128)S(1)} %get-tuple-element.59), channel_id=1, source_target_pairs={{0,96},{8,104},{16,112},{24,120},{32,0},{40,8},{48,16},{56,24},{64... | collective-permute-start | bytes 393224 | tf_op jit(solution)/shard_map/ppermute | solution.py:350
  111.9 5.0 %copy-start.15 = (f32[128,256]{1,0:T(8,128)}, f32[128,256]{1,0:T(8,128)S(1)}, u32[]{:S(2)}) copy-start(f32[128,256]{1,0:T(8,128)S(1)} %collective-permute-done.17.refs_6_) | copy-start | bytes 393220
  111.9 5.0 %copy-start.16 = (f32[128,256]{1,0:T(8,128)}, f32[128,256]{1,0:T(8,128)S(1)}, u32[]{:S(2)}) copy-start(f32[128,256]{1,0:T(8,128)S(1)} %collective-permute-done.18.refs_7_) | copy-start | bytes 393220
  114.6 2.3 copy-start.17
  120.8 7.8 %collective-permute-start.25 = (f32[128,256]{1,0:T(8,128)}, f32[128,256]{1,0:T(8,128)S(1)}, u32[]{:S(2)}, u32[]{:S(2)}) collective-permute-start(f32[128,256]{1,0:T(8,128)} %get-tuple-element.46), channel_id=1, source_target_pairs={{0,8},{8,16},{16,24},{24,0},{32,40},{40,48},{48,56},{56,32},{64,72... | collective-permute-start | bytes 393224 | tf_op jit(solution)/shard_map/ppermute | solution.py:356
  120.9 7.8 %collective-permute-start.26 = (f32[128,256]{1,0:T(8,128)}, f32[128,256]{1,0:T(8,128)S(1)}, u32[]{:S(2)}, u32[]{:S(2)}) collective-permute-start(f32[128,256]{1,0:T(8,128)} %get-tuple-element.46), channel_id=1, source_target_pairs={{0,16},{8,24},{16,0},{24,8},{32,48},{40,56},{48,32},{56,40},{64,80... | collective-permute-start | bytes 393224 | tf_op jit(solution)/shard_map/ppermute | solution.py:356
  124.7 5.2 %collective-permute-start.27 = (f32[128,256]{1,0:T(8,128)}, f32[128,256]{1,0:T(8,128)S(1)}, u32[]{:S(2)}, u32[]{:S(2)}) collective-permute-start(f32[128,256]{1,0:T(8,128)} %get-tuple-element.46), channel_id=1, source_target_pairs={{0,24},{8,0},{16,8},{24,16},{32,56},{40,32},{48,40},{56,48},{64,88... | collective-permute-start | bytes 393224 | tf_op jit(solution)/shard_map/ppermute | solution.py:356
  129.9 42.6 %copy-start.1 = (f32[512,256]{1,0:T(8,128)}, f32[512,256]{1,0:T(8,128)S(1)}, u32[]{:S(2)}) copy-start(f32[512,256]{1,0:T(8,128)S(1)} %constant_dynamic-update-slice_fusion.4.refs_8_) | copy-start | bytes 1572868
  130.0 25.1 %collective-permute-start.28 = (f32[512,256]{1,0:T(8,128)S(1)}, f32[512,256]{1,0:T(8,128)S(1)}, u32[]{:S(2)}, u32[]{:S(2)}) collective-permute-start(f32[512,256]{1,0:T(8,128)S(1)} %constant_dynamic-update-slice_fusion.4.refs_8_), channel_id=1, source_target_pairs={{0,32},{8,40},{16,48},{24,56},{32,64},{40,72},{48,80},{56,88},{64,... | collective-permute-start | bytes 1572872 | tf_op jit(solution)/shard_map/ppermute | solution.py:360
  130.6 18.0 %collective-permute-start.19 = (f32[128,256]{1,0:T(8,128)}, f32[128,256]{1,0:T(8,128)S(1)}, u32[]{:S(2)}, u32[]{:S(2)}) collective-permute-start(f32[128,256]{1,0:T(8,128)} %get-tuple-element.45), channel_id=1, source_target_pairs={{0,32},{8,40},{16,48},{24,56},{32,64},{40,72},{48,80},{56,88},{64,... | collective-permute-start | bytes 393224 | tf_op jit(solution)/shard_map/ppermute | solution.py:355
  130.7 20.3 %collective-permute-start.20 = (f32[128,256]{1,0:T(8,128)}, f32[128,256]{1,0:T(8,128)S(1)}, u32[]{:S(2)}, u32[]{:S(2)}) collective-permute-start(f32[128,256]{1,0:T(8,128)} %get-tuple-element.45), channel_id=1, source_target_pairs={{0,64},{8,72},{16,80},{24,88},{32,96},{40,104},{48,112},{56,120},{... | collective-permute-start | bytes 393224 | tf_op jit(solution)/shard_map/ppermute | solution.py:355
  135.7 15.4 %collective-permute-start.21 = (f32[128,256]{1,0:T(8,128)}, f32[128,256]{1,0:T(8,128)S(1)}, u32[]{:S(2)}, u32[]{:S(2)}) collective-permute-start(f32[128,256]{1,0:T(8,128)} %get-tuple-element.45), channel_id=1, source_target_pairs={{0,96},{8,104},{16,112},{24,120},{32,0},{40,8},{48,16},{56,24},{64... | collective-permute-start | bytes 393224 | tf_op jit(solution)/shard_map/ppermute | solution.py:355
  137.7 34.7 %collective-permute-start.29 = (f32[512,256]{1,0:T(8,128)S(1)}, f32[512,256]{1,0:T(8,128)S(1)}, u32[]{:S(2)}, u32[]{:S(2)}) collective-permute-start(f32[512,256]{1,0:T(8,128)S(1)} %constant_dynamic-update-slice_fusion.4.refs_8_), channel_id=1, source_target_pairs={{0,64},{8,72},{16,80},{24,88},{32,96},{40,104},{48,112},{56,120},{... | collective-permute-start | bytes 1572872 | tf_op jit(solution)/shard_map/ppermute | solution.py:360
  148.6 23.9 %collective-permute-start.30 = (f32[512,256]{1,0:T(8,128)S(1)}, f32[512,256]{1,0:T(8,128)S(1)}, u32[]{:S(2)}, u32[]{:S(2)}) collective-permute-start(f32[512,256]{1,0:T(8,128)S(1)} %constant_dynamic-update-slice_fusion.4.refs_8_), channel_id=1, source_target_pairs={{0,96},{8,104},{16,112},{24,120},{32,0},{40,8},{48,16},{56,24},{64... | collective-permute-start | bytes 1572872 | tf_op jit(solution)/shard_map/ppermute | solution.py:360
  151.1 21.5 %copy-start = (f32[512,256]{1,0:T(8,128)}, f32[512,256]{1,0:T(8,128)S(1)}, u32[]{:S(2)}) copy-start(f32[512,256]{1,0:T(8,128)S(1)} %constant_dynamic-update-slice_fusion.refs_4_) | copy-start | bytes 1572868
  151.1 21.4 %collective-permute-start.22 = (f32[512,256]{1,0:T(8,128)S(1)}, f32[512,256]{1,0:T(8,128)}, u32[]{:S(2)}, u32[]{:S(2)}) collective-permute-start(f32[512,256]{1,0:T(8,128)S(1)} %constant_dynamic-update-slice_fusion.refs_4_), channel_id=1, source_target_pairs={{0,8},{8,16},{16,24},{24,0},{32,40},{40,48},{48,56},{56,32},{64,72... | collective-permute-start | bytes 1572872 | tf_op jit(solution)/shard_map/ppermute | solution.py:359
  153.6 18.9 %collective-permute-start.23 = (f32[512,256]{1,0:T(8,128)S(1)}, f32[512,256]{1,0:T(8,128)}, u32[]{:S(2)}, u32[]{:S(2)}) collective-permute-start(f32[512,256]{1,0:T(8,128)S(1)} %constant_dynamic-update-slice_fusion.refs_4_), channel_id=1, source_target_pairs={{0,16},{8,24},{16,0},{24,8},{32,48},{40,56},{48,32},{56,40},{64,80... | collective-permute-start | bytes 1572872 | tf_op jit(solution)/shard_map/ppermute | solution.py:359
  155.0 17.5 %copy-start.4 = (f32[512,256]{1,0:T(8,128)}, f32[512,256]{1,0:T(8,128)S(1)}, u32[]{:S(2)}) copy-start(f32[512,256]{1,0:T(8,128)S(1)} %collective-permute-done.28.refs_9_) | copy-start | bytes 1572868
  155.0 17.5 %collective-permute-start.24 = (f32[512,256]{1,0:T(8,128)S(1)}, f32[512,256]{1,0:T(8,128)}, u32[]{:S(2)}, u32[]{:S(2)}) collective-permute-start(f32[512,256]{1,0:T(8,128)S(1)} %constant_dynamic-update-slice_fusion.refs_4_), channel_id=1, source_target_pairs={{0,24},{8,0},{16,8},{24,16},{32,56},{40,32},{48,40},{56,48},{64,88... | collective-permute-start | bytes 1572872 | tf_op jit(solution)/shard_map/ppermute | solution.py:359
  180.0 35.8 %collective-permute-start.31 = (f32[1024,256]{1,0:T(8,128)}, f32[1024,256]{1,0:T(8,128)S(1)}, u32[]{:S(2)}, u32[]{:S(2)}) collective-permute-start(f32[1024,256]{1,0:T(8,128)} %get-tuple-element.50), channel_id=1, source_target_pairs={{0,1},{1,0},{2,3},{3,2},{4,5},{5,4},{6,7},{7,6},{8,9},{9,8},{10,11... | collective-permute-start | bytes 3145736 | tf_op jit(solution)/shard_map/ppermute | solution.py:368
  208.2 16.4 %all-to-all-start.3 = ((f32[8,40,256]{2,1,0:T(8,128)}), f32[8,40,256]{2,1,0:T(8,128)S(1)}, u32[]{:S(2)}, u32[]{:S(2)}) async-start(f32[8,40,256]{2,1,0:T(8,128)} %broadcast_in_dim.5), calls=%async_computation.3 | async-start | bytes 655360 | tf_op jit(solution)/shard_map/all_to_all | solution.py:377
  217.1 12.6 %collective-permute-start.32 = (f32[256,256]{1,0:T(8,128)S(1)}, f32[256,256]{1,0:T(8,128)S(1)}, u32[]{:S(2)}, u32[]{:S(2)}) collective-permute-start(f32[256,256]{1,0:T(8,128)S(1)} %get-tuple-element.52), channel_id=1, source_target_pairs={{0,2},{1,3},{2,4},{3,5},{4,6},{5,7},{6,0},{7,1},{8,10},{9,11},{10,... | collective-permute-start | bytes 786440 | tf_op jit(solution)/shard_map/ppermute | solution.py:373
  219.1 16.1 %collective-permute-start.33 = (f32[256,256]{1,0:T(8,128)S(1)}, f32[256,256]{1,0:T(8,128)S(1)}, u32[]{:S(2)}, u32[]{:S(2)}) collective-permute-start(f32[256,256]{1,0:T(8,128)S(1)} %get-tuple-element.54), channel_id=1, source_target_pairs={{0,4},{1,5},{2,6},{3,7},{4,0},{5,1},{6,2},{7,3},{8,12},{9,13},{10,... | collective-permute-start | bytes 786440 | tf_op jit(solution)/shard_map/ppermute | solution.py:373
  221.8 13.5 %collective-permute-start.34 = (f32[256,256]{1,0:T(8,128)S(1)}, f32[256,256]{1,0:T(8,128)S(1)}, u32[]{:S(2)}, u32[]{:S(2)}) collective-permute-start(f32[256,256]{1,0:T(8,128)S(1)} %get-tuple-element.53), channel_id=1, source_target_pairs={{0,6},{1,7},{2,0},{3,1},{4,2},{5,3},{6,4},{7,5},{8,14},{9,15},{10,... | collective-permute-start | bytes 786440 | tf_op jit(solution)/shard_map/ppermute | solution.py:373
  (11 other events, 12.6 us)
where the time goes:
time: 239 us; the launch traced here: 237 us
  starting transfers between devices  87.6 us (37%)
  waiting for transfers between devices  62.7 us (26%)
  blocking collectives  40.8 us (17%)
  Pallas kernels  27.9 us (12%)
  local copies, waits for them, and re-layouts  9.29 us (4%)
  other arithmetic  7.09 us (3%)
    all_to_all x1, blocking collectives, on_device(): sums = lax.all_to_all(sums, 'row', split_axis=0, concat_axis=0, tiled=True)  24.8 us
    ppermute x3, starting transfers between devices, on_device(): lax.ppermute(sum_b[d], 'row', row_hop(0, d))  18.7 us
    all_to_all x1, blocking collectives, on_device(): sums = lax.all_to_all(sums, 'col', split_axis=0, concat_axis=0, tiled=True)  16 us
    pallas_call x2, Pallas kernels, aggregate(): pl.pallas_call(functools.partial(aggregate_kernel, n_src, n_dst), out_sha...  13.3 us
    ppermute x3, waiting for transfers between devices, on_device(): lax.ppermute(grad_a, 'row', row_hop(e, 0))  11.7 us
    all_to_all x1, starting transfers between devices, on_device(): lax.all_to_all(sent, ('row', 'col'), split_axis=0, concat_axis=0, tiled=T...  11.2 us
    ppermute x3, waiting for transfers between devices, on_device(): panel = [own] + [lax.ppermute(own, 'col', col_hop(f, 0)) for f in (1, 2, 3)]  11 us
    ppermute x3, waiting for transfers between devices, on_device(): got_b = [lax.ppermute(half[4 + e], 'row', row_hop(e, 0)) for e in (1, 2, 3)]  10.9 us
  transfers between devices with their start and end apart: 37, of which 17 were waited for; matrix products, arithmetic and copies ran while one was open for 4% of the time, Pallas kernels for 3%

commit v1 on v0

--- a/solution.py
+++ b/solution.py
@@ -26,6 +26,10 @@
 bf16 = jnp.bfloat16
 
 
+def room(mib):
+    return pltpu.CompilerParams(vmem_limit_bytes=mib << 20)
+
+
 def whole():
     return pl.BlockSpec(memory_space=pltpu.VMEM)
 
@@ -55,29 +59,39 @@
     second = lax.broadcasted_iota(jnp.int32, (NODE, NODE), 1)
     earlier = (owner_col == owner_row) & (first < second)
     rank = jnp.sum(earlier.astype(f32), axis=0, keepdims=True).astype(jnp.int32)
-    chosen = (first == owner_row * 2 + rank).astype(f32)
-    sent[:, :F] = jnp.dot(chosen, features[...], precision=precise, preferred_element_type=f32)
-    place = (perm_row[...] & (NODE - 1)).astype(f32)
-    place = jnp.sum(chosen * place, axis=1, keepdims=True)
-    sent[:, F:] = jnp.broadcast_to(place, (NODE, LANES))
+    slot = owner_row[:1] * 2 + rank
+    spot = (perm_row[...] & (NODE - 1)).astype(f32)
+    rows = lax.broadcasted_iota(jnp.int32, (NODE // 2, NODE), 0)
+    for n in range(2):
+        chosen = (rows * 2 + n == slot).astype(f32)
+        sent[:, n, :F] = jnp.dot(
+            chosen, features[...], precision=precise, preferred_element_type=f32
+        )
+        spots = jnp.sum(chosen * spot, axis=1, keepdims=True)
+        sent[:, n, F:] = jnp.broadcast_to(spots, (NODE // 2, LANES))
 
 
 def pack(features, perm):
     return pl.pallas_call(
         pack_kernel,
-        out_shape=jax.ShapeDtypeStruct((NODE, F + LANES), f32),
+        out_shape=jax.ShapeDtypeStruct((NODE // 2, 2, F + LANES), f32),
         in_specs=[whole()] * 2,
         out_specs=whole(),
+        compiler_params=room(8),
         name="pack",
     )(features, perm.reshape(1, NODE))
 
 
 def place_kernel(got, own):
-    place = got[:, F:].astype(jnp.int32)
-    place = jnp.concatenate([place, place], axis=1)
-    second = lax.broadcasted_iota(jnp.int32, (NODE, NODE), 1)
-    chosen = (place == second).astype(f32).T
-    own[...] = jnp.dot(chosen, got[:, :F], precision=precise, preferred_element_type=f32)
+    second = lax.broadcasted_iota(jnp.int32, (NODE // 2, NODE), 1)
+    chosen, rows = [], []
+    for n in range(2):
+        spot = got[:, n, F:].astype(jnp.int32)
+        chosen.append((jnp.concatenate([spot, spot], axis=1) == second).astype(f32))
+        rows.append(got[:, n, :F])
+    chosen = jnp.concatenate(chosen, axis=0).T
+    rows = jnp.concatenate(rows, axis=0)
+    own[...] = jnp.dot(chosen, rows, precision=precise, preferred_element_type=f32)
 
 
 def place(got):
@@ -86,6 +100,7 @@
         out_shape=jax.ShapeDtypeStruct((NODE, F), f32),
         in_specs=[whole()],
         out_specs=whole(),
+        compiler_params=room(8),
         name="place",
     )(got)
 
@@ -122,7 +137,7 @@
 
     return pl.pallas_call(
         functools.partial(prepare_kernel, flip),
-        out_shape=jax.ShapeDtypeStruct((SLOTS, BS, F), bf16),
+        out_shape=pltpu.HBM((SLOTS, BS, F), bf16),
         grid_spec=pltpu.PrefetchScalarGridSpec(
             num_scalar_prefetch=1,
             grid=(SLOTS // STEP,),
@@ -131,8 +146,9 @@
             scratch_shapes=[pltpu.VMEM((STEP * 32, LANES), f32)],
         ),
         cost_estimate=pl.CostEstimate(flops=10**8, bytes_accessed=12 << 20, transcendentals=0),
+        compiler_params=room(8),
         name="prepare_back" if flip else "prepare",
-    )(count, vals)
+    )(count, pltpu.with_memory_space_constraint(vals, pltpu.HBM))
 
 
 def aggregate_kernel(n_src, n_dst, *refs):
@@ -223,12 +239,19 @@
         cost_estimate=pl.CostEstimate(
             flops=2 * SLOTS * BS * F * F, bytes_accessed=16 << 20, transcendentals=0
         ),
-    )(source_at, target_at, count, blocks, *sources)
+        compiler_params=room(16),
+    )(
+        source_at,
+        target_at,
+        count,
+        pltpu.with_memory_space_constraint(blocks, pltpu.HBM),
+        *sources,
+    )
 
 
 def middle_kernel(*refs):
-    parts, (weight, bias, cotangent) = refs[:8], refs[8:11]
-    output, grad_a, grad_b, sums, hidden, turned, strip = refs[11:]
+    where, parts, (weight, bias, cotangent) = refs[0], refs[1:9], refs[9:12]
+    output, grad_a, grad_b, sums, gives, hidden, turned, strip = refs[12:]
     half = NODE // 2
     hidden[:half] = parts[0][...] + parts[1][...] + parts[2][...] + parts[3][...]
     hidden[half:] = parts[4][...] + parts[5][...] + parts[6][...] + parts[7][...]
@@ -260,27 +283,34 @@
                     pl.ds(q * BS + odd * 32, 32), lanes
                 ]
         output[:, lanes] = strip[side * NODE : (side + 1) * NODE]
-    local_w = jnp.dot(rows.T, grad_pre, precision=precise, preferred_element_type=f32)
+    turned[...] = jnp.dot(rows.T, grad_pre, precision=precise, preferred_element_type=f32)
     local_b = jnp.sum(grad_pre, axis=0, keepdims=True)
-    for n in range(COLS):
-        sums[n, 0:32, :] = local_w[n * 32 : (n + 1) * 32]
-        sums[n, 32:, :] = jnp.broadcast_to(local_b, (W_ROWS - 32, F))
-
-
-def middle(parts, weight, bias, cotangent):
+    for f in range(SIDE):
+        ahead = ((where[0] + f) & 3) * 2
+        for side, into in ((where[1], sums), (1 - where[1], gives)):
+            at = pl.multiple_of((ahead + side) * 32, 32)
+            into[f * W_ROWS : f * W_ROWS + 32, :] = turned[pl.ds(at, 32), :]
+            into[f * W_ROWS + 32 : (f + 1) * W_ROWS, :] = jnp.broadcast_to(
+                local_b, (W_ROWS - 32, F)
+            )
+
+
+def middle(parts, weight, bias, cotangent, where):
     return pl.pallas_call(
         middle_kernel,
         out_shape=[
             jax.ShapeDtypeStruct((NODE, F), f32),
             jax.ShapeDtypeStruct((NODE // 2, F), f32),
             jax.ShapeDtypeStruct((NODE // 2, F), f32),
-            jax.ShapeDtypeStruct((COLS, W_ROWS, F), f32),
+            jax.ShapeDtypeStruct((SIDE * W_ROWS, F), f32),
+            jax.ShapeDtypeStruct((SIDE * W_ROWS, F), f32),
         ],
-        in_specs=[whole()] * 11,
-        out_specs=[whole()] * 4,
+        in_specs=[pl.BlockSpec(memory_space=pltpu.SMEM)] + [whole()] * 11,
+        out_specs=[whole()] * 5,
         scratch_shapes=[pltpu.VMEM((NODE, F), f32)] * 2 + [pltpu.VMEM((2 * NODE, LANES), f32)],
+        compiler_params=room(12),
         name="middle",
-    )(*parts, weight, bias.reshape(1, F), cotangent)
+    )(where, *parts, weight, bias.reshape(1, F), cotangent)
 
 
 def on_device(
@@ -320,12 +350,12 @@
     fwd_from = (((my_z - c_z) & 3) * 2 + other) * 4 + c_q
     bwd_to = (other * 4 + ((c_z - my_z) & 3)) * 4 + c_q
 
-    sent = pack(features, loader_perm).reshape(ROWS * COLS, 2, F + LANES)
+    sent = pack(features, loader_perm)
     got = lax.all_to_all(sent, ("row", "col"), split_axis=0, concat_axis=0, tiled=True)
     vals = block_values.reshape(SLOTS, BS * BS)
     fwd_blocks = prepare(vals, count, False)
     got, fwd_blocks = lax.optimization_barrier((got, fwd_blocks))
-    own = place(got.reshape(NODE, F + LANES))
+    own = place(got)
     panel = [own] + [lax.ppermute(own, "col", col_hop(f, 0)) for f in (1, 2, 3)]
     sources = []
     for part in panel:
@@ -350,17 +380,24 @@
     parts = [sum_a[0]] + [lax.ppermute(sum_a[e], "row", row_hop(e, 0)) for e in (1, 2, 3)]
     parts += [sum_b[0]] + [lax.ppermute(sum_b[d], "row", row_hop(0, d)) for d in (1, 2, 3)]
 
-    output, grad_a, grad_b, sums = middle(parts, weight, bias_vector, cotangent)
+    output, grad_a, grad_b, sums, gives = middle(
+        parts, weight, bias_vector, cotangent, jnp.stack([my_z, my_c])
+    )
 
     near_a = [grad_a] + [lax.ppermute(grad_a, "row", row_hop(e, 0)) for e in (1, 2, 3)]
     near_b = [grad_b] + [lax.ppermute(grad_b, "row", row_hop(0, d)) for d in (1, 2, 3)]
     near_a = jnp.concatenate(near_a, axis=0)
     near_b = jnp.concatenate(near_b, axis=0)
-    column = [near_a] + [lax.ppermute(near_a, "row", row_hop(0, d)) for d in (1, 2, 3)]
-    column += [near_b] + [lax.ppermute(near_b, "row", row_hop(e, 0)) for e in (1, 2, 3)]
-
-    sums = lax.all_to_all(sums, "col", split_axis=0, concat_axis=0, tiled=True)
-    sums = jnp.sum(sums, axis=0)
+    near_a, near_b = lax.optimization_barrier((near_a, near_b))
+    far_a = [lax.ppermute(near_a, "row", row_hop(0, d)) for d in (1, 3, 2)]
+    far_b = [lax.ppermute(near_b, "row", row_hop(e, 0)) for e in (1, 3, 2)]
+    column = [near_a, far_a[0], far_a[2], far_a[1], near_b, far_b[0], far_b[2], far_b[1]]
+    column = [pltpu.with_memory_space_constraint(part, pltpu.HBM) for part in column]
+
+    sums = sums + lax.ppermute(gives, "col", col_hop(0, 1))
+    sums = sums.reshape(SIDE, W_ROWS, F)
+    got_w = [lax.ppermute(sums[f], "col", col_hop(f, 0)) for f in (1, 2, 3)]
+    sums = sums[0] + got_w[0] + got_w[1] + got_w[2]
     sums = jnp.broadcast_to(sums[None], (ROWS, W_ROWS, F))
     bwd_from, sums = lax.optimization_barrier((bwd_from, sums))
     sums = lax.all_to_all(sums, "row", split_axis=0, concat_axis=0, tiled=True)

time: 239 us -> 221 us (0.925)
  blocking collectives: 40.8 us -> 24.6 us
  waiting for transfers between devices: 62.7 us -> 73.4 us
  Pallas kernels: 27.9 us -> 20.6 us
  local copies, waits for them, and re-layouts: 9.29 us -> 4.76 us
  other arithmetic: 7.09 us -> 3.5 us
  starting transfers between devices: 87.6 us -> 90.7 us
    ppermute x6 -> x10, waiting for transfers between devices: 0.02 us -> 23.3 us  [the longest x3 17.8 us: on_device(): far_a = [lax.ppermute(near_a, 'row', row_hop(0, d)) for d in (1, 3, 2)]]
    all_to_all x1 -> x0, blocking collectives: 16 us -> none  [on_device(): sums = lax.all_to_all(sums, 'col', split_axis=0, concat_axis=0, tiled=True)]
    ppermute x3, waiting for transfers between devices: 11.7 us -> 2.56 us  [on_device(): lax.ppermute(grad_a, 'row', row_hop(e, 0))]
    ppermute x6 -> x10, starting transfers between devices: 7.58 us -> 16.7 us  [the longest x3 6.76 us: on_device(): got_w = [lax.ppermute(sums[f], 'col', col_hop(f, 0)) for f in (1, 2, 3)]]
    ppermute x3, waiting for transfers between devices: 4.56 us -> 0.08 us  [on_device(): lax.ppermute(grad_b, 'row', row_hop(0, d))]
    all_to_all x1, starting transfers between devices: 7.65 us -> 3.43 us  [on_device(): sums = lax.all_to_all(sums, 'col', split_axis=0, concat_axis=0, tiled=True)]
    pallas_call x2, Pallas kernels: 13.3 us -> 9.22 us  [aggregate(): pl.pallas_call(functools.partial(aggregate_kernel, n_src, n_dst), out_sha...]
    reshape x2 -> x0, local copies, waits for them, and re-layouts: 2.97 us -> none  [the longest x1 1.96 us: on_device(): sent = pack(features, loader_perm).reshape(ROWS * COLS, 2, F + LANES)]
  transfers between devices with their start and end apart: 37 -> 41, of which waited for: 17 -> 22; matrix products, arithmetic and copies ran while one was open for 4% -> 2% of each run, Pallas kernels for 3% -> 3%
where the time goes in v1:
time: 221 us; the launch traced here: 219 us
  starting transfers between devices  90.7 us (41%)
  waiting for transfers between devices  73.4 us (33%)
  blocking collectives  24.6 us (11%)
  Pallas kernels  20.6 us (9%)
  local copies, waits for them, and re-layouts  4.76 us (2%)
  other arithmetic  3.5 us (2%)
    all_to_all x1, blocking collectives, on_device(): sums = lax.all_to_all(sums, 'row', split_axis=0, concat_axis=0, tiled=True)  24.6 us
    ppermute x3, starting transfers between devices, on_device(): lax.ppermute(sum_b[d], 'row', row_hop(0, d))  18.6 us
    ppermute x3, waiting for transfers between devices, on_device(): far_a = [lax.ppermute(near_a, 'row', row_hop(0, d)) for d in (1, 3, 2)]  17.8 us
    all_to_all x1, starting transfers between devices, on_device(): lax.all_to_all(sent, ('row', 'col'), split_axis=0, concat_axis=0, tiled=T...  11.2 us
    ppermute x3, waiting for transfers between devices, on_device(): panel = [own] + [lax.ppermute(own, 'col', col_hop(f, 0)) for f in (1, 2, 3)]  10.8 us
    ppermute x3, waiting for transfers between devices, on_device(): got_b = [lax.ppermute(half[4 + e], 'row', row_hop(e, 0)) for e in (1, 2, 3)]  10.7 us
    ppermute x3, starting transfers between devices, on_device(): got_b = [lax.ppermute(half[4 + e], 'row', row_hop(e, 0)) for e in (1, 2, 3)]  10 us
    ppermute x3, waiting for transfers between devices, on_device(): got_x = [lax.ppermute(sums_x[f], 'col', col_hop(f, 0)) for f in (1, 2, 3)]  9.38 us
  transfers between devices with their start and end apart: 41, of which 22 were waited for; matrix products, arithmetic and copies ran while one was open for 2% of the time, Pallas kernels for 3%

profile of v1, /device:TPU:0, one launch (start us, length us, event | category | flops | bytes accessed | tf_op | source)
XLA Modules:
  0.0 219.1 jit_solution(14050752506624006679)
XLA Ops:
  0.7 0.9 copy-done
  2.3 1.3 pack.1
  3.6 11.2 %all-to-all-start = ((f32[128,2,384]{2,1,0:T(2,128)}), f32[128,2,384]{2,1,0:T(2,128)S(1)}, u32[]{:S(2)}, u32[]{:S(2)}) async-start(f32[128,2,384]{2,1,0:T(2,128)} %pack.1), calls=%async_computation | async-start | bytes 786432 | tf_op jit(solution)/shard_map/all_to_all | solution.py:354
  15.4 3.2 %prepare.1.refs_3_ = bf16[256,64,256]{2,1,0:T(8,128)(2,1)} custom-call(s32[1]{0:T(128)} %bitcast.13.count, f32[256,4096]{1,0:T(8,128)} %bitcast.22), custom_call_target="tpu_custom_call" | custom-call | flops 100000000 | bytes 12582912 | tf_op jit(solution)/shard_map/prepare/pallas_call | solution.py:138
  18.7 8.4 %all-to-all-done.got = f32[128,2,384]{2,1,0:T(2,128)S(1)} async-done(((f32[128,2,384]{2,1,0:T(2,128)}), f32[128,2,384]{2,1,0:T(2,128)S(1)}, u32[]{:S(2)}, u32[]{:S(2)}) %all-to-all-start) | async-done | bytes 393248 | tf_op jit(solution)/shard_map/all_to_all | solution.py:354
  28.0 2.9 %collective-permute-start.3 = (f32[256,256]{1,0:T(8,128)S(1)}, f32[256,256]{1,0:T(8,128)S(1)}, u32[]{:S(2)}, u32[]{:S(2)}) collective-permute-start(f32[256,256]{1,0:T(8,128)S(1)} %place.1.refs_4_), channel_id=1, source_target_pairs={{0,4},{1,5},{2,6},{3,7},{4,0},{5,1},{6,2},{7,3},{8,12},{9,13},{10,... | collective-permute-start | bytes 786440 | tf_op jit(solution)/shard_map/ppermute | solution.py:359
  31.5 10.7 %collective-permute-done.1.refs_6_ = f32[256,256]{1,0:T(8,128)S(1)} collective-permute-done((f32[256,256]{1,0:T(8,128)S(1)}, f32[256,256]{1,0:T(8,128)S(1)}, u32[]{:S(2)}, u32[]{:S(2)}) %collective-permute-start.1) | collective-permute-done | bytes 262176 | tf_op jit(solution)/shard_map/ppermute | solution.py:359
  42.9 0.8 collective-permute-done.2.refs_7_
  44.5 4.0 %shard_map.120 = (f32[512,256]{1,0:T(8,128)S(1)}, f32[512,256]{1,0:T(8,128)S(1)}, f32[512,256]{1,0:T(8,128)S(1)}, f32[512,256]{1,0:T(8,128)S(1)}, f32[512,256]{1...) custom-call(s32[256]{0:T(256)S(1)} %bitcast.17, s32[256]{0:T(256)S(1)} %bitcast.16, ...), custom_call_target="tpu_custom_call" | custom-call | flops 2147483648 | bytes 16777216 | tf_op jit(solution)/shard_map/pallas_call | solution.py:217
  48.4 7.3 %collective-permute-start.13 = (f32[512,256]{1,0:T(8,128)S(1)}, f32[512,256]{1,0:T(8,128)S(1)}, u32[]{:S(2)}, u32[]{:S(2)}) collective-permute-start(f32[512,256]{1,0:T(8,128)S(1)} %get-tuple-element.41), channel_id=1, source_target_pairs={{0,32},{8,40},{16,48},{24,56},{32,64},{40,72},{48,80},{56,88},{64,... | collective-permute-start | bytes 1572872 | tf_op jit(solution)/shard_map/ppermute | solution.py:368
  55.7 2.8 %collective-permute-start.15 = (f32[512,256]{1,0:T(8,128)S(1)}, f32[512,256]{1,0:T(8,128)S(1)}, u32[]{:S(2)}, u32[]{:S(2)}) collective-permute-start(f32[512,256]{1,0:T(8,128)S(1)} %get-tuple-element.43), channel_id=1, source_target_pairs={{0,96},{8,104},{16,112},{24,120},{32,0},{40,8},{48,16},{56,24},{64... | collective-permute-start | bytes 1572872 | tf_op jit(solution)/shard_map/ppermute | solution.py:368
  58.9 2.6 %collective-permute-start.8 = (f32[512,256]{1,0:T(8,128)S(1)}, f32[512,256]{1,0:T(8,128)S(1)}, u32[]{:S(2)}, u32[]{:S(2)}) collective-permute-start(f32[512,256]{1,0:T(8,128)S(1)} %get-tuple-element.38), channel_id=1, source_target_pairs={{0,16},{8,24},{16,0},{24,8},{32,48},{40,56},{48,32},{56,40},{64,80... | collective-permute-start | bytes 1572872 | tf_op jit(solution)/shard_map/ppermute | solution.py:367
  61.4 6.6 %collective-permute-done.13 = f32[512,256]{1,0:T(8,128)S(1)} collective-permute-done((f32[512,256]{1,0:T(8,128)S(1)}, f32[512,256]{1,0:T(8,128)S(1)}, u32[]{:S(2)}, u32[]{:S(2)}) %collective-permute-start.13) | collective-permute-done | bytes 524320 | tf_op jit(solution)/shard_map/ppermute | solution.py:368
  68.0 3.3 %collective-permute-start.9 = (f32[512,256]{1,0:T(8,128)S(1)}, f32[512,256]{1,0:T(8,128)S(1)}, u32[]{:S(2)}, u32[]{:S(2)}) collective-permute-start(f32[512,256]{1,0:T(8,128)S(1)} %get-tuple-element.39), channel_id=1, source_target_pairs={{0,24},{8,0},{16,8},{24,16},{32,56},{40,32},{48,40},{56,48},{64,88... | collective-permute-start | bytes 1572872 | tf_op jit(solution)/shard_map/ppermute | solution.py:367
  71.3 3.8 %prepare_back.1.refs_3_ = bf16[256,64,256]{2,1,0:T(8,128)(2,1)} custom-call(s32[1]{0:T(128)} %bitcast.12.count, f32[256,4096]{1,0:T(8,128)} %bitcast.23), custom_call_target="tpu_custom_call" | custom-call | flops 100000000 | bytes 12582912 | tf_op jit(solution)/shard_map/prepare_back/pallas_call | solution.py:138
  75.1 3.3 %collective-permute-done.14 = f32[512,256]{1,0:T(8,128)S(1)} collective-permute-done((f32[512,256]{1,0:T(8,128)S(1)}, f32[512,256]{1,0:T(8,128)S(1)}, u32[]{:S(2)}, u32[]{:S(2)}) %collective-permute-start.14) | collective-permute-done | bytes 524320 | tf_op jit(solution)/shard_map/ppermute | solution.py:368
  78.4 0.9 collective-permute-done.15
  79.5 15.8 %collective-permute-start.16 = (f32[128,256]{1,0:T(8,128)S(1)}, f32[128,256]{1,0:T(8,128)S(1)}, u32[]{:S(2)}, u32[]{:S(2)}) collective-permute-start(f32[128,256]{1,0:T(8,128)S(1)} %get-tuple-element.63), channel_id=1, source_target_pairs={{0,8},{8,16},{16,24},{24,0},{32,40},{40,48},{48,56},{56,32},{64,72... | collective-permute-start | bytes 393224 | tf_op jit(solution)/shard_map/ppermute | solution.py:381
  95.3 2.8 %collective-permute-start.18 = (f32[128,256]{1,0:T(8,128)S(1)}, f32[128,256]{1,0:T(8,128)S(1)}, u32[]{:S(2)}, u32[]{:S(2)}) collective-permute-start(f32[128,256]{1,0:T(8,128)S(1)} %get-tuple-element.61), channel_id=1, source_target_pairs={{0,24},{8,0},{16,8},{24,16},{32,56},{40,32},{48,40},{56,48},{64,88... | collective-permute-start | bytes 393224 | tf_op jit(solution)/shard_map/ppermute | solution.py:381
  98.3 2.9 %collective-permute-start.11 = (f32[128,256]{1,0:T(8,128)S(1)}, f32[128,256]{1,0:T(8,128)S(1)}, u32[]{:S(2)}, u32[]{:S(2)}) collective-permute-start(f32[128,256]{1,0:T(8,128)S(1)} %get-tuple-element.66), channel_id=1, source_target_pairs={{0,64},{8,72},{16,80},{24,88},{32,96},{40,104},{48,112},{56,120},{... | collective-permute-start | bytes 393224 | tf_op jit(solution)/shard_map/ppermute | solution.py:380
  101.7 4.1 %collective-permute-done.10.refs_2_ = f32[128,256]{1,0:T(8,128)S(1)} collective-permute-done((f32[128,256]{1,0:T(8,128)S(1)}, f32[128,256]{1,0:T(8,128)S(1)}, u32[]{:S(2)}, u32[]{:S(2)}) %collective-permute-start.10) | collective-permute-done | bytes 131104 | tf_op jit(solution)/shard_map/ppermute | solution.py:380
  105.8 0.9 collective-permute-done.12.refs_4_
  106.7 2.3 %middle.1 = (f32[256,256]{1,0:T(8,128)}, f32[128,256]{1,0:T(8,128)S(1)}, f32[128,256]{1,0:T(8,128)S(1)}, f32[160,256]{1,0:T(8,128)S(1)}, f32[160,256]{1,0:T(8,128)S(1)}) custom-call(s32[2]{0:T(128)S(1)} %pad_add_fusion.refs_0_, f32[128,256]{1,0:T(8,128)S(1)} %get-tuple-element.68.refs_1_, f32[128,256]{1,0:T(8,128)S(1)} %collective-permute-done.10.refs_2_, ...), custom_call_target="tpu_custom_call" | custom-call | tf_op jit(solution)/shard_map/middle/pallas_call | solution.py:299
  109.0 2.8 %collective-permute-start.27 = (f32[128,256]{1,0:T(8,128)S(1)}, f32[128,256]{1,0:T(8,128)S(1)}, u32[]{:S(2)}, u32[]{:S(2)}) collective-permute-start(f32[128,256]{1,0:T(8,128)S(1)} %get-tuple-element.50), channel_id=1, source_target_pairs={{0,16},{8,24},{16,0},{24,8},{32,48},{40,56},{48,32},{56,40},{64,80... | collective-permute-start | bytes 393224 | tf_op jit(solution)/shard_map/ppermute | solution.py:388
  113.0 3.5 %collective-permute-start.24 = (f32[128,256]{1,0:T(8,128)S(1)}, f32[128,256]{1,0:T(8,128)S(1)}, u32[]{:S(2)}, u32[]{:S(2)}) collective-permute-start(f32[128,256]{1,0:T(8,128)S(1)} %get-tuple-element.49), channel_id=1, source_target_pairs={{0,64},{8,72},{16,80},{24,88},{32,96},{40,104},{48,112},{56,120},{... | collective-permute-start | bytes 393224 | tf_op jit(solution)/shard_map/ppermute | solution.py:387
  116.6 2.3 %collective-permute-start.25 = (f32[128,256]{1,0:T(8,128)S(1)}, f32[128,256]{1,0:T(8,128)S(1)}, u32[]{:S(2)}, u32[]{:S(2)}) collective-permute-start(f32[128,256]{1,0:T(8,128)S(1)} %get-tuple-element.49), channel_id=1, source_target_pairs={{0,96},{8,104},{16,112},{24,120},{32,0},{40,8},{48,16},{56,24},{64... | collective-permute-start | bytes 393224 | tf_op jit(solution)/shard_map/ppermute | solution.py:387
  119.0 1.9 collective-permute-done.24
  121.6 1.1 collective-permute-start.29
  122.8 1.4 collective-permute-done.19
  124.3 6.6 %collective-permute-start.21 = (f32[40,256]{1,0:T(8,128)S(1)}, f32[40,256]{1,0:T(8,128)S(1)}, u32[]{:S(2)}, u32[]{:S(2)}) collective-permute-start(f32[40,256]{1,0:T(8,128)S(1)} %get-tuple-element.71), channel_id=1, source_target_pairs={{0,4},{1,5},{2,6},{3,7},{4,0},{5,1},{6,2},{7,3},{8,12},{9,13},{10,... | collective-permute-start | bytes 122888 | tf_op jit(solution)/shard_map/ppermute | solution.py:399
  130.9 1.1 collective-permute-start.30
  132.0 2.6 %collective-permute-start.31 = (f32[512,256]{1,0:T(8,128)S(1)}, f32[512,256]{1,0:T(8,128)S(1)}, u32[]{:S(2)}, u32[]{:S(2)}) collective-permute-start(f32[512,256]{1,0:T(8,128)S(1)} %pad_maximum_fusion.refs_4_), channel_id=1, source_target_pairs={{0,24},{8,0},{16,8},{24,16},{32,56},{40,32},{48,40},{56,48},{64,88... | collective-permute-start | bytes 1572872 | tf_op jit(solution)/shard_map/ppermute | solution.py:392
  135.0 4.7 %collective-permute-start.33 = (f32[512,256]{1,0:T(8,128)S(1)}, f32[512,256]{1,0:T(8,128)S(1)}, u32[]{:S(2)}, u32[]{:S(2)}) collective-permute-start(f32[512,256]{1,0:T(8,128)S(1)} %pad_maximum_fusion.1.refs_8_), channel_id=1, source_target_pairs={{0,64},{8,72},{16,80},{24,88},{32,96},{40,104},{48,112},{56,120},{... | collective-permute-start | bytes 1572872 | tf_op jit(solution)/shard_map/ppermute | solution.py:393
  139.8 6.0 %collective-permute-done.30.refs_6_ = f32[512,256]{1,0:T(8,128)S(1)} collective-permute-done((f32[512,256]{1,0:T(8,128)S(1)}, f32[512,256]{1,0:T(8,128)S(1)}, u32[]{:S(2)}, u32[]{:S(2)}) %collective-permute-start.30) | collective-permute-done | bytes 524320 | tf_op jit(solution)/shard_map/ppermute | solution.py:392
  145.9 11.7 %collective-permute-done.31.refs_7_ = f32[512,256]{1,0:T(8,128)S(1)} collective-permute-done((f32[512,256]{1,0:T(8,128)S(1)}, f32[512,256]{1,0:T(8,128)S(1)}, u32[]{:S(2)}, u32[]{:S(2)}) %collective-permute-start.31) | collective-permute-done | bytes 524320 | tf_op jit(solution)/shard_map/ppermute | solution.py:392
  157.6 4.1 %collective-permute-done.33.refs_10_ = f32[512,256]{1,0:T(8,128)S(1)} collective-permute-done((f32[512,256]{1,0:T(8,128)S(1)}, f32[512,256]{1,0:T(8,128)S(1)}, u32[]{:S(2)}, u32[]{:S(2)}) %collective-permute-start.33) | collective-permute-done | bytes 524320 | tf_op jit(solution)/shard_map/ppermute | solution.py:393
  162.8 5.2 %shard_map.121 = (f32[1024,256]{1,0:T(8,128)S(1)}, f32[1024,256]{1,0:T(8,128)S(1)}) custom-call(s32[256]{0:T(256)S(1)} %bitcast.18, s32[256]{0:T(256)S(1)} %bitcast.19, s32[1]{0:T(128)} %bitcast.15.refs_2_, bf16[256,64,256]{2,1,0:T(8,128)(2,1)} %prepare_back.1.refs_3_, f32[512,256]{1,0:T(8,128)} %copy-done.6, f32[512,256]{1,0:T(8,128)} %copy-done.7, ...), custom_call_target="tpu_custom_call" | custom-call | flops 2147483648 | bytes 16777216 | tf_op jit(solution)/shard_map/pallas_call | solution.py:217
  168.0 1.1 collective-permute-start.35
  169.1 24.6 %all_to_all.15 = f32[16,40,256]{2,1,0:T(8,128)S(1)} all-to-all(f32[16,40,256]{2,1,0:T(8,128)S(1)} %broadcast_in_dim.4), channel_id=1, replica_groups=mesh['row'=16,'col'=8] {'row'}, dimensions={0} | all-to-all | bytes 1310720 | tf_op jit(solution)/shard_map/all_to_all | solution.py:403
  194.5 3.4 %all-to-all-start.2 = ((f32[8,40,256]{2,1,0:T(8,128)}), f32[8,40,256]{2,1,0:T(8,128)S(1)}, u32[]{:S(2)}, u32[]{:S(2)}) async-start(f32[8,40,256]{2,1,0:T(8,128)} %broadcast_in_dim.5), calls=%async_computation.2 | async-start | bytes 655360 | tf_op jit(solution)/shard_map/all_to_all | solution.py:414
  198.0 1.2 slice_add_fusion.2
  199.2 2.0 collective-permute-start.36
  201.2 2.7 %collective-permute-start.37 = (f32[256,256]{1,0:T(8,128)S(1)}, f32[256,256]{1,0:T(8,128)S(1)}, u32[]{:S(2)}, u32[]{:S(2)}) collective-permute-start(f32[256,256]{1,0:T(8,128)S(1)} %get-tuple-element.60), channel_id=1, source_target_pairs={{0,4},{1,5},{2,6},{3,7},{4,0},{5,1},{6,2},{7,3},{8,12},{9,13},{10,... | collective-permute-start | bytes 786440 | tf_op jit(solution)/shard_map/ppermute | solution.py:410
  203.9 1.4 collective-permute-start.38
  205.3 1.3 all-to-all-done.2
  208.0 3.8 %collective-permute-done.36 = f32[256,256]{1,0:T(8,128)S(1)} collective-permute-done((f32[256,256]{1,0:T(8,128)S(1)}, f32[256,256]{1,0:T(8,128)S(1)}, u32[]{:S(2)}, u32[]{:S(2)}) %collective-permute-start.36) | collective-permute-done | bytes 262176 | tf_op jit(solution)/shard_map/ppermute | solution.py:410
  211.7 5.6 %collective-permute-done.37 = f32[256,256]{1,0:T(8,128)S(1)} collective-permute-done((f32[256,256]{1,0:T(8,128)S(1)}, f32[256,256]{1,0:T(8,128)S(1)}, u32[]{:S(2)}, u32[]{:S(2)}) %collective-permute-start.37) | collective-permute-done | bytes 262176 | tf_op jit(solution)/shard_map/ppermute | solution.py:410
  217.3 1.7 fusion.2
  (90 shorter events, 10.7 us)
Async XLA Ops:
  0.6 42.2 %copy-start.13 = (s32[1,1,256]{2,1,0:T(1,128)S(1)}, s32[1,1,256]{2,1,0:T(1,128)}, u32[]{:S(2)}) copy-start(s32[1,1,256]{2,1,0:T(1,128)} %param.12) | copy-start | bytes 3076
  2.3 40.6 %copy-start.14 = (s32[1,1,256]{2,1,0:T(1,128)S(1)}, s32[1,1,256]{2,1,0:T(1,128)}, u32[]{:S(2)}) copy-start(s32[1,1,256]{2,1,0:T(1,128)} %param.13) | copy-start | bytes 3076
  3.6 23.5 %all-to-all-start = ((f32[128,2,384]{2,1,0:T(2,128)}), f32[128,2,384]{2,1,0:T(2,128)S(1)}, u32[]{:S(2)}, u32[]{:S(2)}) async-start(f32[128,2,384]{2,1,0:T(2,128)} %pack.1), calls=%async_computation | async-start | bytes 786432 | tf_op jit(solution)/shard_map/all_to_all | solution.py:354
  27.7 14.4 %collective-permute-start.1 = (f32[256,256]{1,0:T(8,128)S(1)}, f32[256,256]{1,0:T(8,128)S(1)}, u32[]{:S(2)}, u32[]{:S(2)}) collective-permute-start(f32[256,256]{1,0:T(8,128)S(1)} %place.1.refs_4_), channel_id=1, source_target_pairs={{0,2},{1,3},{2,4},{3,5},{4,6},{5,7},{6,0},{7,1},{8,10},{9,11},{10,... | collective-permute-start | bytes 786440 | tf_op jit(solution)/shard_map/ppermute | solution.py:359
  28.0 14.1 %collective-permute-start.3 = (f32[256,256]{1,0:T(8,128)S(1)}, f32[256,256]{1,0:T(8,128)S(1)}, u32[]{:S(2)}, u32[]{:S(2)}) collective-permute-start(f32[256,256]{1,0:T(8,128)S(1)} %place.1.refs_4_), channel_id=1, source_target_pairs={{0,4},{1,5},{2,6},{3,7},{4,0},{5,1},{6,2},{7,3},{8,12},{9,13},{10,... | collective-permute-start | bytes 786440 | tf_op jit(solution)/shard_map/ppermute | solution.py:359
  31.0 11.8 %collective-permute-start.5 = (f32[256,256]{1,0:T(8,128)S(1)}, f32[256,256]{1,0:T(8,128)S(1)}, u32[]{:S(2)}, u32[]{:S(2)}) collective-permute-start(f32[256,256]{1,0:T(8,128)S(1)} %place.1.refs_4_), channel_id=1, source_target_pairs={{0,6},{1,7},{2,0},{3,1},{4,2},{5,3},{6,4},{7,5},{8,14},{9,15},{10,... | collective-permute-start | bytes 786440 | tf_op jit(solution)/shard_map/ppermute | solution.py:359
  31.2 11.7 %collective-permute-start = (f32[256,256]{1,0:T(8,128)S(1)}, f32[256,256]{1,0:T(8,128)S(1)}, u32[]{:S(2)}, u32[]{:S(2)}) collective-permute-start(f32[256,256]{1,0:T(8,128)S(1)} %place.1.refs_4_), channel_id=1, source_target_pairs={{0,1},{1,0},{2,3},{3,2},{4,5},{5,4},{6,7},{7,6},{8,9},{9,8},{10,11... | collective-permute-start | bytes 786440 | tf_op jit(solution)/shard_map/ppermute | solution.py:362
  42.2 1.5 collective-permute-start.2
  42.2 1.9 collective-permute-start.4
  42.8 1.7 collective-permute-start.6
  48.4 19.6 %collective-permute-start.13 = (f32[512,256]{1,0:T(8,128)S(1)}, f32[512,256]{1,0:T(8,128)S(1)}, u32[]{:S(2)}, u32[]{:S(2)}) collective-permute-start(f32[512,256]{1,0:T(8,128)S(1)} %get-tuple-element.41), channel_id=1, source_target_pairs={{0,32},{8,40},{16,48},{24,56},{32,64},{40,72},{48,80},{56,88},{64,... | collective-permute-start | bytes 1572872 | tf_op jit(solution)/shard_map/ppermute | solution.py:368
  55.7 22.7 %collective-permute-start.14 = (f32[512,256]{1,0:T(8,128)S(1)}, f32[512,256]{1,0:T(8,128)S(1)}, u32[]{:S(2)}, u32[]{:S(2)}) collective-permute-start(f32[512,256]{1,0:T(8,128)S(1)} %get-tuple-element.42), channel_id=1, source_target_pairs={{0,64},{8,72},{16,80},{24,88},{32,96},{40,104},{48,112},{56,120},{... | collective-permute-start | bytes 1572872 | tf_op jit(solution)/shard_map/ppermute | solution.py:368
  55.7 23.6 %collective-permute-start.15 = (f32[512,256]{1,0:T(8,128)S(1)}, f32[512,256]{1,0:T(8,128)S(1)}, u32[]{:S(2)}, u32[]{:S(2)}) collective-permute-start(f32[512,256]{1,0:T(8,128)S(1)} %get-tuple-element.43), channel_id=1, source_target_pairs={{0,96},{8,104},{16,112},{24,120},{32,0},{40,8},{48,16},{56,24},{64... | collective-permute-start | bytes 1572872 | tf_op jit(solution)/shard_map/ppermute | solution.py:368
  58.5 36.8 %collective-permute-start.7 = (f32[512,256]{1,0:T(8,128)S(1)}, f32[512,256]{1,0:T(8,128)S(1)}, u32[]{:S(2)}, u32[]{:S(2)}) collective-permute-start(f32[512,256]{1,0:T(8,128)S(1)} %get-tuple-element.35), channel_id=1, source_target_pairs={{0,8},{8,16},{16,24},{24,0},{32,40},{40,48},{48,56},{56,32},{64,72... | collective-permute-start | bytes 1572872 | tf_op jit(solution)/shard_map/ppermute | solution.py:367
  58.9 39.2 %collective-permute-start.8 = (f32[512,256]{1,0:T(8,128)S(1)}, f32[512,256]{1,0:T(8,128)S(1)}, u32[]{:S(2)}, u32[]{:S(2)}) collective-permute-start(f32[512,256]{1,0:T(8,128)S(1)} %get-tuple-element.38), channel_id=1, source_target_pairs={{0,16},{8,24},{16,0},{24,8},{32,48},{40,56},{48,32},{56,40},{64,80... | collective-permute-start | bytes 1572872 | tf_op jit(solution)/shard_map/ppermute | solution.py:367
  68.0 30.0 %collective-permute-start.9 = (f32[512,256]{1,0:T(8,128)S(1)}, f32[512,256]{1,0:T(8,128)S(1)}, u32[]{:S(2)}, u32[]{:S(2)}) collective-permute-start(f32[512,256]{1,0:T(8,128)S(1)} %get-tuple-element.39), channel_id=1, source_target_pairs={{0,24},{8,0},{16,8},{24,16},{32,56},{40,32},{48,40},{56,48},{64,88... | collective-permute-start | bytes 1572872 | tf_op jit(solution)/shard_map/ppermute | solution.py:367
  71.3 35.4 %copy-start.1 = (f32[256,256]{1,0:T(8,128)S(1)}, f32[256,256]{1,0:T(8,128)}, u32[]{:S(2)}) copy-start(f32[256,256]{1,0:T(8,128)} %refs_9_.1) | copy-start | bytes 786436
  71.3 35.4 %copy-start.2 = (f32[256,256]{1,0:T(8,128)S(1)}, f32[256,256]{1,0:T(8,128)}, u32[]{:S(2)}) copy-start(f32[256,256]{1,0:T(8,128)} %refs_11_.1) | copy-start | bytes 786436
  71.3 35.4 %copy-start.4 = (f32[256]{0:T(256)S(1)}, f32[256]{0:T(256)}, u32[]{:S(2)}) copy-start(f32[256]{0:T(256)} %param.16) | copy-start | bytes 3076
  79.5 21.7 %collective-permute-start.16 = (f32[128,256]{1,0:T(8,128)S(1)}, f32[128,256]{1,0:T(8,128)S(1)}, u32[]{:S(2)}, u32[]{:S(2)}) collective-permute-start(f32[128,256]{1,0:T(8,128)S(1)} %get-tuple-element.63), channel_id=1, source_target_pairs={{0,8},{8,16},{16,24},{24,0},{32,40},{40,48},{48,56},{56,32},{64,72... | collective-permute-start | bytes 393224 | tf_op jit(solution)/shard_map/ppermute | solution.py:381
  95.3 6.5 %collective-permute-start.17 = (f32[128,256]{1,0:T(8,128)S(1)}, f32[128,256]{1,0:T(8,128)S(1)}, u32[]{:S(2)}, u32[]{:S(2)}) collective-permute-start(f32[128,256]{1,0:T(8,128)S(1)} %get-tuple-element.62), channel_id=1, source_target_pairs={{0,16},{8,24},{16,0},{24,8},{32,48},{40,56},{48,32},{56,40},{64,80... | collective-permute-start | bytes 393224 | tf_op jit(solution)/shard_map/ppermute | solution.py:381
  95.3 6.5 %collective-permute-start.18 = (f32[128,256]{1,0:T(8,128)S(1)}, f32[128,256]{1,0:T(8,128)S(1)}, u32[]{:S(2)}, u32[]{:S(2)}) collective-permute-start(f32[128,256]{1,0:T(8,128)S(1)} %get-tuple-element.61), channel_id=1, source_target_pairs={{0,24},{8,0},{16,8},{24,16},{32,56},{40,32},{48,40},{56,48},{64,88... | collective-permute-start | bytes 393224 | tf_op jit(solution)/shard_map/ppermute | solution.py:381
  98.2 7.7 %collective-permute-start.10 = (f32[128,256]{1,0:T(8,128)S(1)}, f32[128,256]{1,0:T(8,128)S(1)}, u32[]{:S(2)}, u32[]{:S(2)}) collective-permute-start(f32[128,256]{1,0:T(8,128)S(1)} %get-tuple-element.67), channel_id=1, source_target_pairs={{0,32},{8,40},{16,48},{24,56},{32,64},{40,72},{48,80},{56,88},{64,... | collective-permute-start | bytes 393224 | tf_op jit(solution)/shard_map/ppermute | solution.py:380
  98.3 7.6 %collective-permute-start.11 = (f32[128,256]{1,0:T(8,128)S(1)}, f32[128,256]{1,0:T(8,128)S(1)}, u32[]{:S(2)}, u32[]{:S(2)}) collective-permute-start(f32[128,256]{1,0:T(8,128)S(1)} %get-tuple-element.66), channel_id=1, source_target_pairs={{0,64},{8,72},{16,80},{24,88},{32,96},{40,104},{48,112},{56,120},{... | collective-permute-start | bytes 393224 | tf_op jit(solution)/shard_map/ppermute | solution.py:380
  101.2 5.6 %collective-permute-start.12 = (f32[128,256]{1,0:T(8,128)S(1)}, f32[128,256]{1,0:T(8,128)S(1)}, u32[]{:S(2)}, u32[]{:S(2)}) collective-permute-start(f32[128,256]{1,0:T(8,128)S(1)} %get-tuple-element.65), channel_id=1, source_target_pairs={{0,96},{8,104},{16,112},{24,120},{32,0},{40,8},{48,16},{56,24},{64... | collective-permute-start | bytes 393224 | tf_op jit(solution)/shard_map/ppermute | solution.py:380
  109.0 7.6 %collective-permute-start.26 = (f32[128,256]{1,0:T(8,128)S(1)}, f32[128,256]{1,0:T(8,128)S(1)}, u32[]{:S(2)}, u32[]{:S(2)}) collective-permute-start(f32[128,256]{1,0:T(8,128)S(1)} %get-tuple-element.50), channel_id=1, source_target_pairs={{0,8},{8,16},{16,24},{24,0},{32,40},{40,48},{48,56},{56,32},{64,72... | collective-permute-start | bytes 393224 | tf_op jit(solution)/shard_map/ppermute | solution.py:388
  109.0 9.9 %collective-permute-start.27 = (f32[128,256]{1,0:T(8,128)S(1)}, f32[128,256]{1,0:T(8,128)S(1)}, u32[]{:S(2)}, u32[]{:S(2)}) collective-permute-start(f32[128,256]{1,0:T(8,128)S(1)} %get-tuple-element.50), channel_id=1, source_target_pairs={{0,16},{8,24},{16,0},{24,8},{32,48},{40,56},{48,32},{56,40},{64,80... | collective-permute-start | bytes 393224 | tf_op jit(solution)/shard_map/ppermute | solution.py:388
  111.8 7.1 %collective-permute-start.28 = (f32[128,256]{1,0:T(8,128)S(1)}, f32[128,256]{1,0:T(8,128)S(1)}, u32[]{:S(2)}, u32[]{:S(2)}) collective-permute-start(f32[128,256]{1,0:T(8,128)S(1)} %get-tuple-element.50), channel_id=1, source_target_pairs={{0,24},{8,0},{16,8},{24,16},{32,56},{40,32},{48,40},{56,48},{64,88... | collective-permute-start | bytes 393224 | tf_op jit(solution)/shard_map/ppermute | solution.py:388
  112.4 6.6 %collective-permute-start.23 = (f32[128,256]{1,0:T(8,128)S(1)}, f32[128,256]{1,0:T(8,128)S(1)}, u32[]{:S(2)}, u32[]{:S(2)}) collective-permute-start(f32[128,256]{1,0:T(8,128)S(1)} %get-tuple-element.49), channel_id=1, source_target_pairs={{0,32},{8,40},{16,48},{24,56},{32,64},{40,72},{48,80},{56,88},{64,... | collective-permute-start | bytes 393224 | tf_op jit(solution)/shard_map/ppermute | solution.py:387
  113.0 7.9 %collective-permute-start.24 = (f32[128,256]{1,0:T(8,128)S(1)}, f32[128,256]{1,0:T(8,128)S(1)}, u32[]{:S(2)}, u32[]{:S(2)}) collective-permute-start(f32[128,256]{1,0:T(8,128)S(1)} %get-tuple-element.49), channel_id=1, source_target_pairs={{0,64},{8,72},{16,80},{24,88},{32,96},{40,104},{48,112},{56,120},{... | collective-permute-start | bytes 393224 | tf_op jit(solution)/shard_map/ppermute | solution.py:387
  116.6 5.0 %collective-permute-start.25 = (f32[128,256]{1,0:T(8,128)S(1)}, f32[128,256]{1,0:T(8,128)S(1)}, u32[]{:S(2)}, u32[]{:S(2)}) collective-permute-start(f32[128,256]{1,0:T(8,128)S(1)} %get-tuple-element.49), channel_id=1, source_target_pairs={{0,96},{8,104},{16,112},{24,120},{32,0},{40,8},{48,16},{56,24},{64... | collective-permute-start | bytes 393224 | tf_op jit(solution)/shard_map/ppermute | solution.py:387
  119.0 42.8 %copy-start.5 = (f32[512,256]{1,0:T(8,128)}, f32[512,256]{1,0:T(8,128)S(1)}, u32[]{:S(2)}) copy-start(f32[512,256]{1,0:T(8,128)S(1)} %pad_maximum_fusion.1.refs_8_) | copy-start | bytes 1572868
  121.6 40.2 %copy-start.6 = (f32[512,256]{1,0:T(8,128)}, f32[512,256]{1,0:T(8,128)S(1)}, u32[]{:S(2)}) copy-start(f32[512,256]{1,0:T(8,128)S(1)} %pad_maximum_fusion.refs_4_) | copy-start | bytes 1572868
  121.6 18.1 %collective-permute-start.29 = (f32[512,256]{1,0:T(8,128)S(1)}, f32[512,256]{1,0:T(8,128)S(1)}, u32[]{:S(2)}, u32[]{:S(2)}) collective-permute-start(f32[512,256]{1,0:T(8,128)S(1)} %pad_maximum_fusion.refs_4_), channel_id=1, source_target_pairs={{0,8},{8,16},{16,24},{24,0},{32,40},{40,48},{48,56},{56,32},{64,72... | collective-permute-start | bytes 1572872 | tf_op jit(solution)/shard_map/ppermute | solution.py:392
  122.7 1.4 collective-permute-start.19
  124.2 7.9 %collective-permute-start.20 = (f32[40,256]{1,0:T(8,128)S(1)}, f32[40,256]{1,0:T(8,128)S(1)}, u32[]{:S(2)}, u32[]{:S(2)}) collective-permute-start(f32[40,256]{1,0:T(8,128)S(1)} %get-tuple-element.69), channel_id=1, source_target_pairs={{0,2},{1,3},{2,4},{3,5},{4,6},{5,7},{6,0},{7,1},{8,10},{9,11},{10,... | collective-permute-start | bytes 122888 | tf_op jit(solution)/shard_map/ppermute | solution.py:399
  124.3 10.3 %collective-permute-start.21 = (f32[40,256]{1,0:T(8,128)S(1)}, f32[40,256]{1,0:T(8,128)S(1)}, u32[]{:S(2)}, u32[]{:S(2)}) collective-permute-start(f32[40,256]{1,0:T(8,128)S(1)} %get-tuple-element.71), channel_id=1, source_target_pairs={{0,4},{1,5},{2,6},{3,7},{4,0},{5,1},{6,2},{7,3},{8,12},{9,13},{10,... | collective-permute-start | bytes 122888 | tf_op jit(solution)/shard_map/ppermute | solution.py:399
  130.9 4.0 %collective-permute-start.22 = (f32[40,256]{1,0:T(8,128)S(1)}, f32[40,256]{1,0:T(8,128)S(1)}, u32[]{:S(2)}, u32[]{:S(2)}) collective-permute-start(f32[40,256]{1,0:T(8,128)S(1)} %get-tuple-element.70), channel_id=1, source_target_pairs={{0,6},{1,7},{2,0},{3,1},{4,2},{5,3},{6,4},{7,5},{8,14},{9,15},{10,... | collective-permute-start | bytes 122888 | tf_op jit(solution)/shard_map/ppermute | solution.py:399
  130.9 14.9 %collective-permute-start.30 = (f32[512,256]{1,0:T(8,128)S(1)}, f32[512,256]{1,0:T(8,128)S(1)}, u32[]{:S(2)}, u32[]{:S(2)}) collective-permute-start(f32[512,256]{1,0:T(8,128)S(1)} %pad_maximum_fusion.refs_4_), channel_id=1, source_target_pairs={{0,16},{8,24},{16,0},{24,8},{32,48},{40,56},{48,32},{56,40},{64,80... | collective-permute-start | bytes 1572872 | tf_op jit(solution)/shard_map/ppermute | solution.py:392
  132.0 25.6 %collective-permute-start.31 = (f32[512,256]{1,0:T(8,128)S(1)}, f32[512,256]{1,0:T(8,128)S(1)}, u32[]{:S(2)}, u32[]{:S(2)}) collective-permute-start(f32[512,256]{1,0:T(8,128)S(1)} %pad_maximum_fusion.refs_4_), channel_id=1, source_target_pairs={{0,24},{8,0},{16,8},{24,16},{32,56},{40,32},{48,40},{56,48},{64,88... | collective-permute-start | bytes 1572872 | tf_op jit(solution)/shard_map/ppermute | solution.py:392
  134.6 23.0 %collective-permute-start.32 = (f32[512,256]{1,0:T(8,128)S(1)}, f32[512,256]{1,0:T(8,128)S(1)}, u32[]{:S(2)}, u32[]{:S(2)}) collective-permute-start(f32[512,256]{1,0:T(8,128)S(1)} %pad_maximum_fusion.1.refs_8_), channel_id=1, source_target_pairs={{0,32},{8,40},{16,48},{24,56},{32,64},{40,72},{48,80},{56,88},{64,... | collective-permute-start | bytes 1572872 | tf_op jit(solution)/shard_map/ppermute | solution.py:393
  135.0 26.8 %collective-permute-start.33 = (f32[512,256]{1,0:T(8,128)S(1)}, f32[512,256]{1,0:T(8,128)S(1)}, u32[]{:S(2)}, u32[]{:S(2)}) collective-permute-start(f32[512,256]{1,0:T(8,128)S(1)} %pad_maximum_fusion.1.refs_8_), channel_id=1, source_target_pairs={{0,64},{8,72},{16,80},{24,88},{32,96},{40,104},{48,112},{56,120},{... | collective-permute-start | bytes 1572872 | tf_op jit(solution)/shard_map/ppermute | solution.py:393
  139.7 22.0 %collective-permute-start.34 = (f32[512,256]{1,0:T(8,128)S(1)}, f32[512,256]{1,0:T(8,128)S(1)}, u32[]{:S(2)}, u32[]{:S(2)}) collective-permute-start(f32[512,256]{1,0:T(8,128)S(1)} %pad_maximum_fusion.1.refs_8_), channel_id=1, source_target_pairs={{0,96},{8,104},{16,112},{24,120},{32,0},{40,8},{48,16},{56,24},{64... | collective-permute-start | bytes 1572872 | tf_op jit(solution)/shard_map/ppermute | solution.py:393
  168.0 29.9 %collective-permute-start.35 = (f32[1024,256]{1,0:T(8,128)S(1)}, f32[1024,256]{1,0:T(8,128)}, u32[]{:S(2)}, u32[]{:S(2)}) collective-permute-start(f32[1024,256]{1,0:T(8,128)S(1)} %get-tuple-element.56), channel_id=1, source_target_pairs={{0,1},{1,0},{2,3},{3,2},{4,5},{5,4},{6,7},{7,6},{8,9},{9,8},{10,11... | collective-permute-start | bytes 3145736 | tf_op jit(solution)/shard_map/ppermute | solution.py:405
  194.5 12.1 %all-to-all-start.2 = ((f32[8,40,256]{2,1,0:T(8,128)}), f32[8,40,256]{2,1,0:T(8,128)S(1)}, u32[]{:S(2)}, u32[]{:S(2)}) async-start(f32[8,40,256]{2,1,0:T(8,128)} %broadcast_in_dim.5), calls=%async_computation.2 | async-start | bytes 655360 | tf_op jit(solution)/shard_map/all_to_all | solution.py:414
  199.2 12.5 %collective-permute-start.36 = (f32[256,256]{1,0:T(8,128)S(1)}, f32[256,256]{1,0:T(8,128)S(1)}, u32[]{:S(2)}, u32[]{:S(2)}) collective-permute-start(f32[256,256]{1,0:T(8,128)S(1)} %get-tuple-element.58), channel_id=1, source_target_pairs={{0,2},{1,3},{2,4},{3,5},{4,6},{5,7},{6,0},{7,1},{8,10},{9,11},{10,... | collective-permute-start | bytes 786440 | tf_op jit(solution)/shard_map/ppermute | solution.py:410
  201.2 16.2 %collective-permute-start.37 = (f32[256,256]{1,0:T(8,128)S(1)}, f32[256,256]{1,0:T(8,128)S(1)}, u32[]{:S(2)}, u32[]{:S(2)}) collective-permute-start(f32[256,256]{1,0:T(8,128)S(1)} %get-tuple-element.60), channel_id=1, source_target_pairs={{0,4},{1,5},{2,6},{3,7},{4,0},{5,1},{6,2},{7,3},{8,12},{9,13},{10,... | collective-permute-start | bytes 786440 | tf_op jit(solution)/shard_map/ppermute | solution.py:410
  203.9 13.5 %collective-permute-start.38 = (f32[256,256]{1,0:T(8,128)S(1)}, f32[256,256]{1,0:T(8,128)S(1)}, u32[]{:S(2)}, u32[]{:S(2)}) collective-permute-start(f32[256,256]{1,0:T(8,128)S(1)} %get-tuple-element.59), channel_id=1, source_target_pairs={{0,6},{1,7},{2,0},{3,1},{4,2},{5,3},{6,4},{7,5},{8,14},{9,15},{10,... | collective-permute-start | bytes 786440 | tf_op jit(solution)/shard_map/ppermute | solution.py:410
  (8 other events, 49.9 us)
